TPU v7x, 32 devices: a whole 2x2x4 slice. The times are simulated.
32 devices in a mesh: ax: 4 (over x, core), xs: 8 (over z, y).
Axes of the slice: x: 2, y: 2, z: 4, core: 2. Of those that a mesh axis runs over, the one named last changes fastest.
Arguments:
- concentrations_before: float32 [9, 48, 32, 1024], P(None, 'ax', 'xs'), may hold values from 0.05 to 1
- thermal_field_before: float32 [48, 32, 1024], P('ax', 'xs'), may hold values from 0.8 to 2.5
- flow_speed_vector: float32 [3, 48, 32, 1024], P(None, 'ax', 'xs'), may hold values from -4 to 4
- gap_indicator: int32 [48, 32, 1024], P('ax', 'xs'), may hold values 0 or 1
- destination_slice: int32 [48], replicated, may hold values from 0 to 47, as said below
- reaction_rate_constant: float32 [9], replicated, may hold values from 0.5 to 4
- threshold_kelvin: float32 [9], replicated, may hold values from 0.5 to 3
- reaction_coefficient_matrix: float32 [9, 9], replicated, may hold values from -2 to 2
- energy_release: float32 [9], replicated, may hold values from -4 to 4
- viewer_picture: float32 [32, 1024], P('xs', 'ax'), may hold values from 0 to 1.5
Outputs:
- concentrations_after: float32 [9, 48, 32, 1024], P(None, 'ax', 'xs')
- thermal_field_after: float32 [48, 32, 1024], P('ax', 'xs')
- image_error: float32 [32, 1024], P('xs', 'ax')
Inputs may be any that keep to these rules, and one draw needn't show every extreme that they name: destination_slice[p] = p minus the number of 2 distinct merge positions (each in 1 to 47) at or before p, one of which lies in 1 to 12; so destination_slice is nondecreasing, lies in [p - 2, p], and each new plane from 0 to 45 receives between one and 3 old planes (more than two only where merge positions are adjacent).
All inputs are finite; a program needn't handle non-finite values. No bound on the sum of `gap_indicator` on one device may be relied on, other than what follows from the above.
Results may differ from a plain program's by a relative error of at most 0.000053.
Values sent between devices are 32-bit elements; how exact they have to be, the bound alone decides.
No kernel may reach another device: no remote copies, remote signals or barrier semaphores. Data moves between devices by JAX's collectives and lax.ppermute only.
A program may use at most 64 MiB of HBM per device.

v0:
```python
import functools

import jax
import jax.numpy as jnp
from jax import lax
from jax.experimental import pallas as pl
from jax.experimental.pallas import tpu as pltpu
from jax.sharding import PartitionSpec as P


SPECIES = 9
FIELDS = SPECIES + 1
GLOW = 4
SHIFT = 2
LANES = 128
GRANT = 16 << 20
FLOPS = 10**8


def tiled(x):
    *lead, rows, columns = x.shape
    n = len(lead)
    split = x.reshape(*lead, rows, columns // LANES, LANES)
    order = tuple(range(n)) + (n + 1, n, n + 2)
    return split.transpose(order).reshape(*lead, rows * columns // LANES, LANES)


def untiled(x, rows):
    *lead, height, _ = x.shape
    n = len(lead)
    split = x.reshape(*lead, height // rows, rows, LANES)
    order = tuple(range(n)) + (n + 1, n, n + 2)
    return split.transpose(order).reshape(*lead, rows, height // rows * LANES)


def swaps(count, offset):
    pairs = []
    for i in range(offset, count - 1, 2):
        pairs += [(i, i + 1), (i + 1, i)]
    return pairs


def remap_weights(owner, plane):
    total = owner.shape[0]
    inside = jnp.logical_and(plane >= 0, plane < total)
    hits = []
    for k in range(SHIFT + 1):
        p = plane + k
        mine = owner[jnp.clip(p, 0, total - 1)] == plane
        hits.append(jnp.where(inside & (p < total) & mine, 1.0, 0.0))
    count = hits[0] + hits[1] + hits[2]
    share = jnp.where(count > 2.5, 1.0 / 3.0, jnp.where(count > 1.5, 0.5, 1.0))
    kept = jnp.where(jnp.logical_and(inside, count < 0.5), 1.0, 0.0)
    return hits[0] * share + kept, hits[1] * share, hits[2] * share


def mix(weights, values):
    return weights[0] * values[0] + weights[1] * values[1] + weights[2] * values[2]


def old_field(c, t, f):
    return t if f == SPECIES else c.at[f]


def edge_starts(rows):
    even = lax.rem(lax.axis_index("xs"), 2) == 0
    return jnp.where(even, rows - 1, 0), jnp.where(even, 0, rows - 1)


def send_kernel(rows, c, t, owner, to_even, to_odd, up_even, up_odd, old, shares, table, sems):
    planes, height, _ = t.shape
    tiles = height // rows
    copies = [pltpu.make_async_copy(owner, table, sems.at[FIELDS])]
    for f in range(FIELDS):
        copies.append(pltpu.make_async_copy(old_field(c, t, f), old.at[f], sems.at[f]))
    for copy in copies:
        copy.start()
    copies[0].wait()
    first = lax.axis_index("ax") * planes
    weights = []
    for j in range(planes + 2):
        weights.append(remap_weights(table, first - 1 + j))
        for k, w in enumerate(weights[j]):
            shares[j, k] = jnp.full((8, LANES), w, jnp.float32)
    starts = edge_starts(rows)
    for f in range(FIELDS):
        copies[f + 1].wait()
        for start, out in zip(starts, (to_even, to_odd)):
            edge = [old[f, p, pl.ds(start, tiles, stride=rows), :] for p in range(planes)]
            for j in range(planes - SHIFT):
                out[f, j] = mix(weights[j + 1], edge[j : j + 3])
    even = lax.rem(lax.axis_index("ax"), 2) == 0
    depth = SHIFT + 1
    for f in range(FIELDS):
        up_even[f] = old[f, pl.ds(jnp.where(even, planes - depth, 0), depth)]
        up_odd[f] = old[f, pl.ds(jnp.where(even, 0, planes - depth), depth)]


def late_kernel(rows, shares, old, got_even, got_odd, to_even, to_odd):
    planes, height = old.shape[1:3]
    tiles = height // rows
    starts = edge_starts(rows)
    even = lax.rem(lax.axis_index("ax"), 2) == 0
    weights = [
        [shares[planes - SHIFT + 1 + j, k, :tiles] for k in range(SHIFT + 1)] for j in range(SHIFT)
    ]
    for f in range(FIELDS):
        for start, out in zip(starts, (to_even, to_odd)):
            where = pl.ds(start, tiles, stride=rows)
            edge = [old[f, planes - SHIFT + p, where, :] for p in range(SHIFT)]
            for p in range(SHIFT):
                edge.append(jnp.where(even, got_even[f, p, where, :], got_odd[f, p, where, :]))
            for j in range(SHIFT):
                out[f, j] = mix(weights[j], edge[j : j + 3])


def fetch(sources, targets, sems):
    copies = [
        pltpu.make_async_copy(source, target, sems.at[i])
        for i, (source, target) in enumerate(zip(sources, targets))
    ]
    for copy in copies:
        copy.start()
    return copies


def cells(rows, p, b, numbers, held, flow, gap, out):
    rate, threshold, matrix, release = numbers
    lane = lax.broadcasted_iota(jnp.int32, (8, LANES), 1)
    row = lax.rem(lax.broadcasted_iota(jnp.int32, (8, LANES), 0), rows)
    first_lane, last_lane = lane == 0, lane == LANES - 1
    here = pl.ds(8 * b, 8)
    va, vy, vz = (0.1 * flow[d, p, here] for d in range(3))
    up_y = jnp.where(row == rows - 1, 0.0, 0.1 - vy)
    low_y = jnp.where(row == 0, 0.0, 0.1 + vy)
    up_a, low_a, up_z, low_z = 0.1 - va, 0.1 + va, 0.1 - vz, 0.1 + vz

    def at(f, plane, offset):
        return held[f, plane, pl.ds(8 + 8 * b + offset, 8)]

    flux, mid = [], []
    for f in range(FIELDS):
        m = at(f, p + 1, 0)
        above_z = jnp.where(first_lane, at(f, p + 1, rows), m)
        below_z = jnp.where(last_lane, at(f, p + 1, -rows), m)
        flux.append(
            0.4 * m
            + up_a * at(f, p + 2, 0)
            + low_a * at(f, p, 0)
            + up_y * at(f, p + 1, 1)
            + low_y * at(f, p + 1, -1)
            + up_z * pltpu.roll(above_z, LANES - 1, 1)
            + low_z * pltpu.roll(below_z, 1, 1)
        )
        mid.append(m)
    inverse = 1.0 / mid[SPECIES]
    rates = []
    for r in range(SPECIES):
        speed = rate[r] * jnp.exp(-threshold[r] * inverse)
        rates.append(speed * mid[r] * mid[(r + 1) % SPECIES])
    half_gas = 0.5 * (1 - gap[p, here]).astype(jnp.float32)
    for f in range(FIELDS):
        parts = [
            (release[r] if f == SPECIES else matrix[f, r]) * rates[r] for r in range(SPECIES)
        ]
        out[f, p, here] = flux[f] + half_gas * sum(parts[1:], parts[0])


def inner_kernel(
    rows, shares, old, flow_in, gap_in, rate, threshold, matrix, release,
    held, out, flow, gap, s_rate, s_threshold, s_matrix, s_release, sems,
):
    planes, height = old.shape[1:3]
    numbers = (s_rate, s_threshold, s_matrix, s_release)
    copies = fetch(
        (flow_in, gap_in, rate, threshold, matrix, release), (flow, gap) + numbers, sems
    )
    zeros = jnp.zeros((8, LANES), jnp.float32)

    def remap(j, carry):
        for f in range(FIELDS):
            held[f, j + 1, 0:8] = zeros
            held[f, j + 1, 8 + height : 16 + height] = zeros
            for b in range(height // 8):
                held[f, j + 1, pl.ds(8 + 8 * b, 8)] = mix(
                    [shares[j + 1, k] for k in range(SHIFT + 1)],
                    [old[f, j + k, pl.ds(8 * b, 8)] for k in range(SHIFT + 1)],
                )
        return carry

    lax.fori_loop(0, planes - SHIFT, remap, 0)
    for copy in copies:
        copy.wait()

    def step(p, carry):
        for b in range(height // 8):
            cells(rows, p, b, numbers, held, flow, gap, out)
        return carry

    lax.fori_loop(1, planes - SHIFT - 1, step, 0)


def outer_kernel(
    rows, shares, old, got_even, got_odd, held_in, out_in, flow, gap, rate, threshold, matrix,
    release, held, out, s_rate, s_threshold, s_matrix, s_release, sems,
):
    planes, height = old.shape[1:3]
    numbers = (s_rate, s_threshold, s_matrix, s_release)
    copies = fetch((rate, threshold, matrix, release), numbers, sems)
    even = lax.rem(lax.axis_index("ax"), 2) == 0
    zeros = jnp.zeros((8, LANES), jnp.float32)

    def remap(f, carry):
        for j in range(planes - SHIFT, planes):
            held[f, j + 1, 0:8] = zeros
            held[f, j + 1, 8 + height : 16 + height] = zeros
        for b in range(height // 8):
            here, body = pl.ds(8 * b, 8), pl.ds(8 + 8 * b, 8)

            def pair(p, flip):
                one, two = got_even[f, p, here], got_odd[f, p, here]
                return jnp.where(even, two, one) if flip else jnp.where(even, one, two)

            def put(j, values):
                held[f, j + 1, body] = mix([shares[j + 1, k] for k in range(SHIFT + 1)], values)

            put(-1, [pair(SHIFT, True), old[f, 0, here], old[f, 1, here]])
            chain = [old[f, planes - SHIFT + p, here] for p in range(SHIFT)]
            chain += [pair(p, False) for p in range(SHIFT + 1)]
            for j in range(SHIFT + 1):
                put(planes - SHIFT + j, chain[j : j + 3])
        return carry

    lax.fori_loop(0, FIELDS, remap, 0)
    for copy in copies:
        copy.wait()

    def step(i, carry):
        p = jnp.where(i == 0, 0, planes - SHIFT - 2 + i)
        for b in range(height // 8):
            cells(rows, p, b, numbers, held, flow, gap, out)
        return carry

    lax.fori_loop(0, SHIFT + 2, step, 0)


def add_rows(rows, f, p, even, flow, one, two, out):
    tiles = one.shape[0]
    for y, sign, value in (
        (rows - 1, -0.1, jnp.where(even, one, two)),
        (0, 0.1, jnp.where(even, two, one)),
    ):
        where = pl.ds(y, tiles, stride=rows)
        out[f, p, where, :] = out[f, p, where, :] + (0.1 + sign * flow[1, p, where, :]) * value


def light(f_out, gap, p):
    gas = (1 - gap[p]).astype(jnp.float32)
    return gas * f_out[GLOW, p] * f_out[SPECIES, p]


def most_kernel(rows, part_in, flow, gap, one, two, part, final, thermal, glow, sems):
    planes, _ = part.shape[1:3]
    even = lax.rem(lax.axis_index("xs"), 2) == 0
    ready = planes - SHIFT
    order = [GLOW, SPECIES] + [f for f in range(SPECIES) if f != GLOW]
    copies = []
    for f in order:
        for p in range(ready):
            add_rows(rows, f, p, even, flow, one[f, p], two[f, p], part)
        target = thermal if f == SPECIES else final.at[f]
        here = pl.ds(0, ready)
        copies.append(pltpu.make_async_copy(part.at[f, here], target.at[here], sems.at[f]))
        copies[-1].start()
    total = light(part, gap, 0)
    for p in range(1, ready):
        total += light(part, gap, p)
    glow[...] = total
    for copy in copies:
        copy.wait()


def glow_kernel(rows, scale, part, flow, gap, one, two, glow, *rest):
    *outs, edge, picture = rest
    planes, height = part.shape[1:3]
    even = lax.rem(lax.axis_index("xs"), 2) == 0
    total = glow[...]
    for p in range(SHIFT):
        for i, f in enumerate((GLOW, SPECIES)):
            edge[i, p] = part[f, planes - SHIFT + p]
            tiles = one.shape[2]
            for y, sign, value in (
                (rows - 1, -0.1, jnp.where(even, one[f, p], two[f, p])),
                (0, 0.1, jnp.where(even, two[f, p], one[f, p])),
            ):
                where = pl.ds(y, tiles, stride=rows)
                slope = 0.1 + sign * flow[1, planes - SHIFT + p, where, :]
                edge[i, p, where, :] = edge[i, p, where, :] + slope * value
        gas = (1 - gap[planes - SHIFT + p]).astype(jnp.float32)
        total += gas * edge[0, p] * edge[1, p]
    picture[...] = total * scale
    split_rows(picture, outs, height, lax.axis_size("ax") // 2)


def split_rows(picture, outs, height, stage):
    if len(outs) == 1:
        outs[0][...] = picture[...]
        return
    half = height // 2
    upper = lax.rem(lax.axis_index("ax") // stage, 2)
    for keep, out in zip((upper, 1 - upper), outs):
        out[...] = picture[pl.ds(pl.multiple_of(keep * half, 8), half), :]


def join_kernel(stage, kept, got, *rest):
    *outs, picture = rest
    picture[...] = kept[...] + got[...]
    split_rows(picture, outs, picture.shape[0], stage)


def rest_kernel(rows, part_in, flow, one, two, final_in, thermal_in, part, final, thermal, sems):
    planes, _ = part.shape[1:3]
    even = lax.rem(lax.axis_index("xs"), 2) == 0
    here = pl.ds(planes - SHIFT, SHIFT)
    copies = []
    for f in range(FIELDS):
        for p in range(SHIFT):
            add_rows(rows, f, planes - SHIFT + p, even, flow, one[f, p], two[f, p], part)
        target = thermal if f == SPECIES else final.at[f]
        copies.append(pltpu.make_async_copy(part.at[f, here], target.at[here], sems.at[f]))
        copies[-1].start()
    for copy in copies:
        copy.wait()


def call(kernel, args, outs, scratch=(), aliases=None, us=1):
    spaces = {"v": pltpu.VMEM, "h": pltpu.HBM}
    return pl.pallas_call(
        kernel,
        out_shape=tuple(spaces[m](shape, jnp.float32) if m != "g" else jax.ShapeDtypeStruct(shape, jnp.int32) for shape, m in outs),
        in_specs=[pl.BlockSpec(memory_space=spaces[m]) for _, m in args],
        out_specs=tuple(pl.BlockSpec(memory_space=spaces.get(m, pltpu.VMEM)) for _, m in outs),
        scratch_shapes=list(scratch),
        input_output_aliases=aliases or {},
        cost_estimate=pl.CostEstimate(flops=int(us * FLOPS), bytes_accessed=0, transcendentals=0),
        compiler_params=pltpu.CompilerParams(vmem_limit_bytes=GRANT),
    )(*(pltpu.with_memory_space_constraint(a, spaces[m]) for a, m in args))


def per_device(c, t, flow, gap, owner, rate, threshold, matrix, release, viewer):
    rows = t.shape[1]
    c, t, flow, gap = (tiled(x) for x in (c, t, flow, gap))
    planes, height, _ = t.shape
    tiles = height // rows
    count = lax.axis_size("ax")
    early = ((FIELDS, planes - SHIFT, tiles, LANES), "v")
    late = ((FIELDS, SHIFT, tiles, LANES), "v")
    ends = ((FIELDS, SHIFT + 1, height, LANES), "v")
    whole = ((FIELDS, planes, height, LANES), "v")
    padded = ((FIELDS, planes + 2, height + 16, LANES), "v")
    numbers = [(x, "h") for x in (rate, threshold, matrix, release)]
    number_slots = [pltpu.SMEM(x.shape, x.dtype) for x, _ in numbers]
    sems = pltpu.SemaphoreType.DMA
    bind = functools.partial

    to_even, to_odd, up_even, up_odd, old, shares = call(
        bind(send_kernel, rows),
        [(c, "h"), (t, "h"), (owner, "h")],
        [early, early, ends, ends, whole, ((planes + 2, SHIFT + 1, 8, LANES), "v")],
        [pltpu.SMEM(owner.shape, owner.dtype), sems((FIELDS + 1,))],
    )
    xs_even, xs_odd = swaps(lax.axis_size("xs"), 0), swaps(lax.axis_size("xs"), 1)
    ax_even, ax_odd = swaps(count, 0), swaps(count, 1)
    em = lax.ppermute(to_even, "xs", xs_even)
    om = lax.ppermute(to_odd, "xs", xs_odd)
    got_even = lax.ppermute(up_even, "ax", ax_even)
    got_odd = lax.ppermute(up_odd, "ax", ax_odd)
    held, part, flow_v, gap_v = call(
        bind(inner_kernel, rows),
        [(shares, "v"), (old, "v"), (flow, "h"), (gap, "h")] + numbers,
        [padded, whole, (flow.shape, "v"), (gap.shape, "g")],
        number_slots + [sems((6,))], us=4,
    )
    late_even, late_odd = call(
        bind(late_kernel, rows),
        [(shares, "v"), (old, "v"), (got_even, "v"), (got_odd, "v")], [late, late],
    )
    el = lax.ppermute(late_even, "xs", xs_even)
    ol = lax.ppermute(late_odd, "xs", xs_odd)
    held, part = call(
        bind(outer_kernel, rows),
        [(shares, "v"), (old, "v"), (got_even, "v"), (got_odd, "v"), (held, "v"), (part, "v"),
         (flow_v, "v"), (gap_v, "v")] + numbers,
        [padded, whole], number_slots + [sems((4,))], {4: 0, 5: 1}, us=2,
    )
    final_shape = (SPECIES, planes, height, LANES)
    thermal_shape = (planes, height, LANES)
    part, final, thermal, glow = call(
        bind(most_kernel, rows),
        [(part, "v"), (flow_v, "v"), (gap_v, "v"), (em, "v"), (om, "v")],
        [whole, (final_shape, "h"), (thermal_shape, "h"), ((height, LANES), "v")],
        [sems((FIELDS,))], {0: 0}, us=2,
    )
    direct = count & (count - 1) == 0 and tiles % count == 0
    pieces = 2 if direct else 1
    glows = call(
        bind(glow_kernel, rows, 1.0 / owner.shape[0]),
        [(part, "v"), (flow_v, "v"), (gap_v, "v"), (el, "v"), (ol, "v"), (glow, "v")],
        [((height // pieces, LANES), "v")] * pieces,
        [pltpu.VMEM((2, SHIFT, height, LANES), jnp.float32), pltpu.VMEM((height, LANES), jnp.float32)],
    )
    part, final, thermal = call(
        bind(rest_kernel, rows),
        [(part, "v"), (flow_v, "v"), (el, "v"), (ol, "v"), (final, "h"), (thermal, "h")],
        [whole, (final_shape, "h"), (thermal_shape, "h")],
        [sems((FIELDS,))], {0: 0, 4: 1, 5: 2},
    )
    place = lax.axis_index("ax")
    if direct:
        stage = count // 2
        while True:
            pairs = [(i, i ^ stage) for i in range(count)]
            kept, got = glows[0], lax.ppermute(glows[1], "ax", pairs)
            if stage == 1:
                break
            stage //= 2
            size = kept.shape[0]
            glows = call(
                bind(join_kernel, stage), [(kept, "v"), (got, "v")],
                [((size // 2, LANES), "v")] * 2, [pltpu.VMEM((size, LANES), jnp.float32)],
            )
        error = untiled(kept + got - tiled(viewer), rows)
    else:
        picture = lax.psum(untiled(glows[0], rows), "ax")
        columns = picture.shape[1] // count
        mine = lax.dynamic_slice_in_dim(picture, place * columns, columns, 1)
        error = mine - viewer
    return untiled(final, rows), untiled(thermal, rows), error


def solution(mesh):
    volume, field = P(None, "ax", "xs", None), P("ax", "xs", None)
    in_specs = (volume, field, volume, field, P(), P(), P(), P(), P(), P("xs", "ax"))
    return jax.shard_map(
        per_device,
        mesh=mesh,
        in_specs=in_specs,
        out_specs=(volume, field, P("xs", "ax")),
        check_vma=False,
    )
```

profile of v0, /device:TPU:0, one launch (start us, length us, event | category | flops | bytes accessed | tf_op | source)
XLA Modules:
  0.0 33.3 jit_solution(5136924387784425989)
XLA Ops:
  0.6 1.8 %shard_map.121 = (f32[10,10,8,128]{3,2,1,0:T(8,128)S(1)}, f32[10,10,8,128]{3,2,1,0:T(8,128)S(1)}, f32[10,3,32,128]{3,2,1,0:T(8,128)S(1)}, f32[10,3,32,128]{3,2,1...) custom-call(f32[9,12,32,128]{3,2,1,0:T(8,128)} %bitcast.41, f32[12,32,128]{2,1,0:T(8,128)} %bitcast.44, ...), custom_call_target="tpu_custom_call" | custom-call | flops 100000000 | tf_op jit(solution)/shard_map/pallas_call | solution.py:338
  2.4 0.6 %collective-permute-start = (f32[10,3,32,128]{3,2,1,0:T(8,128)S(1)}, f32[10,3,32,128]{3,2,1,0:T(8,128)S(1)}, u32[]{:S(2)}, u32[]{:S(2)}) collective-permute-start(f32[10,3,32,128]{3,2,1,0:T(8,128)S(1)} %get-tuple-element.28), channel_id=1, source_target_pairs={{0,8},{8,0},{16,24},{24,16},{1,9},{9,1},{17,25},{25,17},{2,10},{10... | collective-permute-start | bytes 1474568 | tf_op jit(solution)/shard_map/ppermute | solution.py:376
  2.9 0.7 %collective-permute-start.1 = (f32[10,3,32,128]{3,2,1,0:T(8,128)S(1)}, f32[10,3,32,128]{3,2,1,0:T(8,128)S(1)}, u32[]{:S(2)}, u32[]{:S(2)}) collective-permute-start(f32[10,3,32,128]{3,2,1,0:T(8,128)S(1)} %get-tuple-element.29), channel_id=1, source_target_pairs={{8,16},{16,8},{9,17},{17,9},{10,18},{18,10},{11,19},{19,11},{12,20... | collective-permute-start | bytes 1474568 | tf_op jit(solution)/shard_map/ppermute | solution.py:377
  3.6 2.6 %collective-permute-start.2 = (f32[10,10,8,128]{3,2,1,0:T(8,128)S(1)}, f32[10,10,8,128]{3,2,1,0:T(8,128)S(1)}, u32[]{:S(2)}, u32[]{:S(2)}) collective-permute-start(f32[10,10,8,128]{3,2,1,0:T(8,128)S(1)} %get-tuple-element.35), channel_id=1, source_target_pairs={{0,1},{1,0},{2,3},{3,2},{4,5},{5,4},{6,7},{7,6},{8,9},{9,8},{10,11... | collective-permute-start | bytes 1228808 | tf_op jit(solution)/shard_map/ppermute | solution.py:374
  6.2 0.7 %collective-permute-start.3 = (f32[10,10,8,128]{3,2,1,0:T(8,128)S(1)}, f32[10,10,8,128]{3,2,1,0:T(8,128)S(1)}, u32[]{:S(2)}, u32[]{:S(2)}) collective-permute-start(f32[10,10,8,128]{3,2,1,0:T(8,128)S(1)} %get-tuple-element.36), channel_id=1, source_target_pairs={{1,2},{2,1},{3,4},{4,3},{5,6},{6,5},{9,10},{10,9},{11,12},{12,11},... | collective-permute-start | bytes 1228808 | tf_op jit(solution)/shard_map/ppermute | solution.py:375
  6.9 0.0 collective-permute-done.got_even
  6.9 0.0 collective-permute-done.1.got_odd
  6.9 0.1 shard_map.125
  7.0 4.3 %collective-permute-start.4 = (f32[10,2,8,128]{3,2,1,0:T(8,128)S(1)}, f32[10,2,8,128]{3,2,1,0:T(8,128)S(1)}, u32[]{:S(2)}, u32[]{:S(2)}) collective-permute-start(f32[10,2,8,128]{3,2,1,0:T(8,128)S(1)} %get-tuple-element.38), channel_id=1, source_target_pairs={{0,1},{1,0},{2,3},{3,2},{4,5},{5,4},{6,7},{7,6},{8,9},{9,8},{10,11... | collective-permute-start | bytes 245768 | tf_op jit(solution)/shard_map/ppermute | solution.py:388
  11.3 0.7 %collective-permute-start.5 = (f32[10,2,8,128]{3,2,1,0:T(8,128)S(1)}, f32[10,2,8,128]{3,2,1,0:T(8,128)S(1)}, u32[]{:S(2)}, u32[]{:S(2)}) collective-permute-start(f32[10,2,8,128]{3,2,1,0:T(8,128)S(1)} %get-tuple-element.39), channel_id=1, source_target_pairs={{1,2},{2,1},{3,4},{4,3},{5,6},{6,5},{9,10},{10,9},{11,12},{12,11},... | collective-permute-start | bytes 245768 | tf_op jit(solution)/shard_map/ppermute | solution.py:389
  12.0 3.5 %shard_map.122 = (f32[10,14,48,128]{3,2,1,0:T(8,128)S(1)}, f32[10,12,32,128]{3,2,1,0:T(8,128)S(1)}, f32[3,12,32,128]{3,2,1,0:T(8,128)S(1)}, s32[12,32,128]{2,1,0:T(8,128)S(1)}) custom-call(f32[14,3,8,128]{3,2,1,0:T(8,128)S(1)} %get-tuple-element.26.shares, f32[10,12,32,128]{3,2,1,0:T(8,128)S(1)} %get-tuple-element.27.old, f32[3,12,32,128]{3,2,1,0:T(8,128)} %bitcast.42, ...), custom_call_target="tpu_custom_call" | custom-call | flops 400000000 | tf_op jit(solution)/shard_map/pallas_call | solution.py:338
  15.5 2.0 %shard_map.123 = (f32[10,14,48,128]{3,2,1,0:T(8,128)S(1)}, f32[10,12,32,128]{3,2,1,0:T(8,128)S(1)}) custom-call(f32[14,3,8,128]{3,2,1,0:T(8,128)S(1)} %get-tuple-element.26.shares, f32[10,12,32,128]{3,2,1,0:T(8,128)S(1)} %get-tuple-element.27.old, ...), custom_call_target="tpu_custom_call", output_to_operand_aliasing={{0}: (4, {}), {1}: (5, {})} | custom-call | flops 200000000 | tf_op jit(solution)/shard_map/pallas_call | solution.py:338
  17.5 7.3 %collective-permute-done.2.one = f32[10,10,8,128]{3,2,1,0:T(8,128)S(1)} collective-permute-done((f32[10,10,8,128]{3,2,1,0:T(8,128)S(1)}, f32[10,10,8,128]{3,2,1,0:T(8,128)S(1)}, u32[]{:S(2)}, u32[]{:S(2)}) %collective-permute-start.2) | collective-permute-done | bytes 409632 | tf_op jit(solution)/shard_map/ppermute | solution.py:374
  24.8 0.0 collective-permute-done.3.two
  24.8 1.3 %shard_map.124 = (f32[10,12,32,128]{3,2,1,0:T(8,128)S(1)}, f32[9,12,32,128]{3,2,1,0:T(8,128)}, f32[12,32,128]{2,1,0:T(8,128)}, f32[32,128]{1,0:T(8,128)S(1)}) custom-call(f32[10,12,32,128]{3,2,1,0:T(8,128)S(1)} %get-tuple-element.34.part_in, f32[3,12,32,128]{3,2,1,0:T(8,128)S(1)} %get-tuple-element.32.flow, ...), custom_call_target="tpu_custom_call", output_to_operand_aliasing={{0}: (0, {})} | custom-call | flops 200000000 | tf_op jit(solution)/shard_map/pallas_call | solution.py:338
  26.0 0.5 %collective-permute-done.4.one = f32[10,2,8,128]{3,2,1,0:T(8,128)S(1)} collective-permute-done((f32[10,2,8,128]{3,2,1,0:T(8,128)S(1)}, f32[10,2,8,128]{3,2,1,0:T(8,128)S(1)}, u32[]{:S(2)}, u32[]{:S(2)}) %collective-permute-start.4) | collective-permute-done | bytes 81952 | tf_op jit(solution)/shard_map/ppermute | solution.py:388
  26.5 0.0 collective-permute-done.5.two
  26.6 3.3 %collective-permute-start.6 = (f32[16,128]{1,0:T(8,128)S(1)}, f32[16,128]{1,0:T(8,128)S(1)}, u32[]{:S(2)}, u32[]{:S(2)}) collective-permute-start(f32[16,128]{1,0:T(8,128)S(1)} %get-tuple-element.46), channel_id=1, source_target_pairs={{0,16},{8,24},{16,0},{24,8},{1,17},{9,25},{17,1},{25,9},{2,18},{10... | collective-permute-start | bytes 24584 | tf_op jit(solution)/shard_map/ppermute | solution.py:423
  29.9 1.6 %collective-permute-done.6.got = f32[16,128]{1,0:T(8,128)S(1)} collective-permute-done((f32[16,128]{1,0:T(8,128)S(1)}, f32[16,128]{1,0:T(8,128)S(1)}, u32[]{:S(2)}, u32[]{:S(2)}) %collective-permute-start.6) | collective-permute-done | bytes 8224 | tf_op jit(solution)/shard_map/ppermute | solution.py:423
  31.5 0.1 collective-permute-start.7
  31.7 0.0 copy-start
  31.7 0.8 %shard_map.126 = (f32[10,12,32,128]{3,2,1,0:T(8,128)S(1)}, f32[9,12,32,128]{3,2,1,0:T(8,128)}, f32[12,32,128]{2,1,0:T(8,128)}) custom-call(f32[10,12,32,128]{3,2,1,0:T(8,128)S(1)} %get-tuple-element.37.part_in.part, f32[3,12,32,128]{3,2,1,0:T(8,128)S(1)} %get-tuple-element.32.flow, ...), custom_call_target="tpu_custom_call", output_to_operand_aliasing={{0}: (0, {}), {1}: (4, {}), {2}: (5, {})} | custom-call | flops 100000000 | tf_op jit(solution)/shard_map/pallas_call | solution.py:338
  32.5 0.2 collective-permute-done.7
  32.7 0.0 copy-done
  32.7 0.6 %add_subtract_fusion = f32[8,128]{1,0:T(8,128)} fusion(f32[8,128]{1,0:T(8,128)S(1)} %bitcast.46, f32[8,128]{1,0:T(8,128)S(1)} %get-tuple-element.47, f32[8,128]{1,0:T(8,128)S(1)} %collective-permute-done.7), kind=kLoop, calls=%fused_computation | loop fusion | flops 2048 | bytes 16384 | tf_op jit(solution)/shard_map/sub | solution.py:432
  (2 shorter events, 0.0 us)
Async XLA Ops:
  2.4 4.5 %collective-permute-start = (f32[10,3,32,128]{3,2,1,0:T(8,128)S(1)}, f32[10,3,32,128]{3,2,1,0:T(8,128)S(1)}, u32[]{:S(2)}, u32[]{:S(2)}) collective-permute-start(f32[10,3,32,128]{3,2,1,0:T(8,128)S(1)} %get-tuple-element.28), channel_id=1, source_target_pairs={{0,8},{8,0},{16,24},{24,16},{1,9},{9,1},{17,25},{25,17},{2,10},{10... | collective-permute-start | bytes 1474568 | tf_op jit(solution)/shard_map/ppermute | solution.py:376
  2.9 4.0 %collective-permute-start.1 = (f32[10,3,32,128]{3,2,1,0:T(8,128)S(1)}, f32[10,3,32,128]{3,2,1,0:T(8,128)S(1)}, u32[]{:S(2)}, u32[]{:S(2)}) collective-permute-start(f32[10,3,32,128]{3,2,1,0:T(8,128)S(1)} %get-tuple-element.29), channel_id=1, source_target_pairs={{8,16},{16,8},{9,17},{17,9},{10,18},{18,10},{11,19},{19,11},{12,20... | collective-permute-start | bytes 1474568 | tf_op jit(solution)/shard_map/ppermute | solution.py:377
  3.6 21.1 %collective-permute-start.2 = (f32[10,10,8,128]{3,2,1,0:T(8,128)S(1)}, f32[10,10,8,128]{3,2,1,0:T(8,128)S(1)}, u32[]{:S(2)}, u32[]{:S(2)}) collective-permute-start(f32[10,10,8,128]{3,2,1,0:T(8,128)S(1)} %get-tuple-element.35), channel_id=1, source_target_pairs={{0,1},{1,0},{2,3},{3,2},{4,5},{5,4},{6,7},{7,6},{8,9},{9,8},{10,11... | collective-permute-start | bytes 1228808 | tf_op jit(solution)/shard_map/ppermute | solution.py:374
  6.2 18.5 %collective-permute-start.3 = (f32[10,10,8,128]{3,2,1,0:T(8,128)S(1)}, f32[10,10,8,128]{3,2,1,0:T(8,128)S(1)}, u32[]{:S(2)}, u32[]{:S(2)}) collective-permute-start(f32[10,10,8,128]{3,2,1,0:T(8,128)S(1)} %get-tuple-element.36), channel_id=1, source_target_pairs={{1,2},{2,1},{3,4},{4,3},{5,6},{6,5},{9,10},{10,9},{11,12},{12,11},... | collective-permute-start | bytes 1228808 | tf_op jit(solution)/shard_map/ppermute | solution.py:375
  7.0 19.5 %collective-permute-start.4 = (f32[10,2,8,128]{3,2,1,0:T(8,128)S(1)}, f32[10,2,8,128]{3,2,1,0:T(8,128)S(1)}, u32[]{:S(2)}, u32[]{:S(2)}) collective-permute-start(f32[10,2,8,128]{3,2,1,0:T(8,128)S(1)} %get-tuple-element.38), channel_id=1, source_target_pairs={{0,1},{1,0},{2,3},{3,2},{4,5},{5,4},{6,7},{7,6},{8,9},{9,8},{10,11... | collective-permute-start | bytes 245768 | tf_op jit(solution)/shard_map/ppermute | solution.py:388
  11.3 15.2 %collective-permute-start.5 = (f32[10,2,8,128]{3,2,1,0:T(8,128)S(1)}, f32[10,2,8,128]{3,2,1,0:T(8,128)S(1)}, u32[]{:S(2)}, u32[]{:S(2)}) collective-permute-start(f32[10,2,8,128]{3,2,1,0:T(8,128)S(1)} %get-tuple-element.39), channel_id=1, source_target_pairs={{1,2},{2,1},{3,4},{4,3},{5,6},{6,5},{9,10},{10,9},{11,12},{12,11},... | collective-permute-start | bytes 245768 | tf_op jit(solution)/shard_map/ppermute | solution.py:389
  26.6 5.0 %collective-permute-start.6 = (f32[16,128]{1,0:T(8,128)S(1)}, f32[16,128]{1,0:T(8,128)S(1)}, u32[]{:S(2)}, u32[]{:S(2)}) collective-permute-start(f32[16,128]{1,0:T(8,128)S(1)} %get-tuple-element.46), channel_id=1, source_target_pairs={{0,16},{8,24},{16,0},{24,8},{1,17},{9,25},{17,1},{25,9},{2,18},{10... | collective-permute-start | bytes 24584 | tf_op jit(solution)/shard_map/ppermute | solution.py:423
  31.5 1.2 %collective-permute-start.7 = (f32[8,128]{1,0:T(8,128)S(1)}, f32[8,128]{1,0:T(8,128)S(1)}, u32[]{:S(2)}, u32[]{:S(2)}) collective-permute-start(f32[8,128]{1,0:T(8,128)S(1)} %get-tuple-element.48), channel_id=1, source_target_pairs={{0,8},{8,0},{16,24},{24,16},{1,9},{9,1},{17,25},{25,17},{2,10},{10... | collective-permute-start | bytes 12296 | tf_op jit(solution)/shard_map/ppermute | solution.py:423
  31.7 1.1 %copy-start = (f32[4,256]{1,0:T(4,128)S(1)}, f32[4,256]{1,0:T(4,128)}, u32[]{:S(2)}) copy-start(f32[4,256]{1,0:T(4,128)} %param.19) | copy-start | bytes 12292
where the time goes:
time: 33.9 us; the launch traced here: 33.3 us
  starting transfers between devices  12.9 us (38%)
  waiting for transfers between devices  9.63 us (28%)
  Pallas kernels  9.41 us (28%)
  between operations  0.73 us (2%)
  other arithmetic  0.6 us (2%)
    pallas_call x8, Pallas kernels, call(): pl.pallas_call(kernel, out_shape=tuple((spaces[m](shape, jnp.float32) if...  9.41 us
    ppermute x1, waiting for transfers between devices, per_device(): em = lax.ppermute(to_even, 'xs', xs_even)  7.28 us
    ppermute x1, starting transfers between devices, per_device(): el = lax.ppermute(late_even, 'xs', xs_even)  4.33 us
    ppermute x2, starting transfers between devices, per_device(): kept, got = (glows[0], lax.ppermute(glows[1], 'ax', pairs))  3.46 us
    ppermute x1, starting transfers between devices, per_device(): em = lax.ppermute(to_even, 'xs', xs_even)  2.59 us
    ppermute x2, waiting for transfers between devices, per_device(): kept, got = (glows[0], lax.ppermute(glows[1], 'ax', pairs))  1.86 us
    ppermute x1, starting transfers between devices, per_device(): got_odd = lax.ppermute(up_odd, 'ax', ax_odd)  0.68 us
  transfers between devices with their start and end apart: 8, of which 4 were waited for; matrix products, arithmetic and copies ran while one was open for 0% of the time, Pallas kernels for 23%

commit v1 on v0

v1 whole, which is shorter than its diff:
```python
import functools

import jax
import jax.numpy as jnp
from jax import lax
from jax.experimental import pallas as pl
from jax.experimental.pallas import tpu as pltpu
from jax.sharding import PartitionSpec as P


SPECIES = 9
FIELDS = SPECIES + 1
GLOW = 4
ORDER = (GLOW, SPECIES) + tuple(f for f in range(SPECIES) if f != GLOW)
EARLY = 5
SHIFT = 2
LANES = 128
GRANT = 16 << 20
FLOPS = 10**8


def tiled(x):
    *lead, rows, columns = x.shape
    n = len(lead)
    split = x.reshape(*lead, rows, columns // LANES, LANES)
    order = tuple(range(n)) + (n + 1, n, n + 2)
    return split.transpose(order).reshape(*lead, rows * columns // LANES, LANES)


def untiled(x, rows):
    *lead, height, _ = x.shape
    n = len(lead)
    split = x.reshape(*lead, height // rows, rows, LANES)
    order = tuple(range(n)) + (n + 1, n, n + 2)
    return split.transpose(order).reshape(*lead, rows, height // rows * LANES)


def swaps(slabs, count, offset):
    pairs = []
    for slab in range(slabs):
        alone = set(range(count))
        for i in range(offset, count - 1, 2):
            pairs += [(slab * count + i, slab * count + i + 1)]
            pairs += [(slab * count + i + 1, slab * count + i)]
            alone -= {i, i + 1}
        if slabs % 2 == 0:
            pairs += [(slab * count + i, (slab ^ 1) * count + i) for i in sorted(alone)]
    return pairs


def ring(count, distance):
    return [(i, (i + distance) % count) for i in range(count)]


def remap_weights(owner, plane):
    total = owner.shape[0]
    inside = jnp.logical_and(plane >= 0, plane < total)
    hits = []
    for k in range(SHIFT + 1):
        p = plane + k
        mine = owner[jnp.clip(p, 0, total - 1)] == plane
        hits.append(jnp.where(inside & (p < total) & mine, 1.0, 0.0))
    count = hits[0] + hits[1] + hits[2]
    share = jnp.where(count > 2.5, 1.0 / 3.0, jnp.where(count > 1.5, 0.5, 1.0))
    kept = jnp.where(jnp.logical_and(inside, count < 0.5), 1.0, 0.0)
    return hits[0] * share + kept, hits[1] * share, hits[2] * share


def mix(weights, values):
    return weights[0] * values[0] + weights[1] * values[1] + weights[2] * values[2]


def old_field(c, t, f):
    return t if f == SPECIES else c.at[f]


def edge_starts(rows):
    even = lax.rem(lax.axis_index("xs"), 2) == 0
    return jnp.where(even, rows - 1, 0), jnp.where(even, 0, rows - 1)


def rows_sent(planes):
    ready = planes - SHIFT
    ends = range(ready, planes)
    first = [(f, p) for f in ORDER[:EARLY] for p in range(ready)]
    middle = [(f, p) for f in ORDER[:2] for p in ends]
    last = [(f, p) for f in ORDER[EARLY:] for p in range(ready)]
    last_late = [(f, p) for f in ORDER[2:] for p in ends]
    return first, middle, last, last_late


def load_fields(c, t, fields, old, sems):
    copies = {}
    for f in fields:
        copies[f] = pltpu.make_async_copy(old_field(c, t, f), old.at[f], sems.at[f])
        copies[f].start()
    return copies


def edge_rows(rows, f, listed, old, weights, outs):
    planes, height = old.shape[1:3]
    tiles = height // rows
    for start, out in zip(edge_starts(rows), outs):
        edge = [old[f, p, pl.ds(start, tiles, stride=rows), :] for p in range(planes)]
        for j in range(planes - SHIFT):
            out[listed.index((f, j))] = mix(weights[j + 1], edge[j : j + 3])


def send_kernel(rows, c, t, owner, to_even, to_odd, old, shares, table, sems):
    planes = t.shape[0]
    wanted = pltpu.make_async_copy(owner, table, sems.at[FIELDS])
    wanted.start()
    copies = load_fields(c, t, ORDER[:EARLY], old, sems)
    wanted.wait()
    first = lax.axis_index("ax") * planes
    weights = []
    for j in range(planes + 2):
        weights.append(remap_weights(table, first - 1 + j))
        for k, w in enumerate(weights[j]):
            shares[j, k] = jnp.full((8, LANES), w, jnp.float32)
    for f in ORDER[:EARLY]:
        copies[f].wait()
        edge_rows(rows, f, rows_sent(planes)[0], old, weights, (to_even, to_odd))


def more_kernel(
    rows, c, t, shares, old_in, last_even, last_odd, lips, up, down, old, sems,
):
    planes, height, _ = t.shape
    tiles = height // rows
    copies = load_fields(c, t, ORDER[EARLY:], old, sems)
    weights = [[shares[j, k, :tiles] for k in range(SHIFT + 1)] for j in range(planes + 2)]
    for f in ORDER:
        if f in copies:
            copies[f].wait()
            edge_rows(rows, f, rows_sent(planes)[2], old, weights, (last_even, last_odd))
        up[f] = old[f, 0 : SHIFT + 1]
        for p in range(SHIFT):
            for i, y in enumerate((0, rows - 1)):
                lips[(f * SHIFT + p) * 2 + i] = old[f, p, pl.ds(y, tiles, stride=rows), :]
        down[f] = old[f, planes - 1]


def late_kernel(
    rows, shares, old, lips, last_even_in, last_odd_in, to_even, to_odd, last_even, last_odd,
):
    planes, height = old.shape[1:3]
    tiles = height // rows
    starts = edge_starts(rows)
    weights = [
        [shares[planes - SHIFT + 1 + j, k, :tiles] for k in range(SHIFT + 1)] for j in range(SHIFT)
    ]
    _, middle, last, last_late = rows_sent(planes)
    for f in range(FIELDS):
        glows = f in ORDER[:2]
        listed = middle if glows else last + last_late
        for start, out in zip(starts, (to_even, to_odd) if glows else (last_even, last_odd)):
            where = pl.ds(start, tiles, stride=rows)
            edge = [old[f, planes - SHIFT + p, where, :] for p in range(SHIFT)]
            for p in range(SHIFT):
                low, high = (lips[(f * SHIFT + p) * 2 + i] for i in range(2))
                edge.append(jnp.where(start == 0, low, high))
            for j in range(SHIFT):
                out[listed.index((f, planes - SHIFT + j))] = mix(weights[j], edge[j : j + 3])


def fetch(sources, targets, sems):
    copies = [
        pltpu.make_async_copy(source, target, sems.at[i])
        for i, (source, target) in enumerate(zip(sources, targets))
    ]
    for copy in copies:
        copy.start()
    return copies


def cells(rows, p, b, numbers, held, flow, gap, out):
    rate, threshold, matrix, release = numbers
    lane = lax.broadcasted_iota(jnp.int32, (8, LANES), 1)
    row = lax.rem(lax.broadcasted_iota(jnp.int32, (8, LANES), 0), rows)
    first_lane, last_lane = lane == 0, lane == LANES - 1
    here = pl.ds(8 * b, 8)
    va, vy, vz = (0.1 * flow[d, p, here] for d in range(3))
    up_y = jnp.where(row == rows - 1, 0.0, 0.1 - vy)
    low_y = jnp.where(row == 0, 0.0, 0.1 + vy)
    up_a, low_a, up_z, low_z = 0.1 - va, 0.1 + va, 0.1 - vz, 0.1 + vz

    def at(f, plane, offset):
        return held[f, plane, pl.ds(8 + 8 * b + offset, 8)]

    flux, mid = [], []
    for f in range(FIELDS):
        m = at(f, p + 1, 0)
        above_z = jnp.where(first_lane, at(f, p + 1, rows), m)
        below_z = jnp.where(last_lane, at(f, p + 1, -rows), m)
        flux.append(
            0.4 * m
            + up_a * at(f, p + 2, 0)
            + low_a * at(f, p, 0)
            + up_y * at(f, p + 1, 1)
            + low_y * at(f, p + 1, -1)
            + up_z * pltpu.roll(above_z, LANES - 1, 1)
            + low_z * pltpu.roll(below_z, 1, 1)
        )
        mid.append(m)
    inverse = 1.0 / mid[SPECIES]
    rates = []
    for r in range(SPECIES):
        speed = rate[r] * jnp.exp(-threshold[r] * inverse)
        rates.append(speed * mid[r] * mid[(r + 1) % SPECIES])
    half_gas = 0.5 * (1 - gap[p, here]).astype(jnp.float32)
    for f in range(FIELDS):
        parts = [
            (release[r] if f == SPECIES else matrix[f, r]) * rates[r] for r in range(SPECIES)
        ]
        out[f, p, here] = flux[f] + half_gas * sum(parts[1:], parts[0])


def inner_kernel(
    rows, shares, old, flow_in, gap_in, rate, threshold, matrix, release,
    held, out, flow, gap, s_rate, s_threshold, s_matrix, s_release, sems,
):
    planes, height = old.shape[1:3]
    numbers = (s_rate, s_threshold, s_matrix, s_release)
    copies = fetch(
        (flow_in, gap_in, rate, threshold, matrix, release), (flow, gap) + numbers, sems
    )
    zeros = jnp.zeros((8, LANES), jnp.float32)

    def remap(j, carry):
        for f in range(FIELDS):
            held[f, j + 1, 0:8] = zeros
            held[f, j + 1, 8 + height : 16 + height] = zeros
            for b in range(height // 8):
                held[f, j + 1, pl.ds(8 + 8 * b, 8)] = mix(
                    [shares[j + 1, k] for k in range(SHIFT + 1)],
                    [old[f, j + k, pl.ds(8 * b, 8)] for k in range(SHIFT + 1)],
                )
        return carry

    lax.fori_loop(0, planes - SHIFT, remap, 0)
    for f in range(FIELDS):
        for b in range(height // 8):
            for j in (0, planes - SHIFT + 1):
                held[f, j, pl.ds(8 + 8 * b, 8)] = zeros
    for copy in copies:
        copy.wait()

    def step(p, carry):
        for b in range(height // 8):
            cells(rows, p, b, numbers, held, flow, gap, out)
        return carry

    lax.fori_loop(0, planes - SHIFT, step, 0)


def outer_kernel(
    rows, shares, old, upper, lower, held_in, out_in, flow, gap, rate, threshold, matrix,
    release, held, out, s_rate, s_threshold, s_matrix, s_release, sems,
):
    planes, height = old.shape[1:3]
    numbers = (s_rate, s_threshold, s_matrix, s_release)
    copies = fetch((rate, threshold, matrix, release), numbers, sems)
    zeros = jnp.zeros((8, LANES), jnp.float32)

    def remap(f, carry):
        for j in range(planes - SHIFT, planes):
            held[f, j + 1, 0:8] = zeros
            held[f, j + 1, 8 + height : 16 + height] = zeros
        for b in range(height // 8):
            here, body = pl.ds(8 * b, 8), pl.ds(8 + 8 * b, 8)

            def put(j, values):
                held[f, j + 1, body] = mix([shares[j + 1, k] for k in range(SHIFT + 1)], values)

            put(-1, [lower[f, here], old[f, 0, here], old[f, 1, here]])
            chain = [old[f, planes - SHIFT + p, here] for p in range(SHIFT)]
            chain += [upper[f, p, here] for p in range(SHIFT + 1)]
            for j in range(SHIFT + 1):
                put(planes - SHIFT + j, chain[j : j + 3])
        return carry

    lax.fori_loop(0, FIELDS, remap, 0)
    for copy in copies:
        copy.wait()

    for b in range(height // 8):
        here, body = pl.ds(8 * b, 8), pl.ds(8 + 8 * b, 8)
        for p, j, sign in ((0, 0, 0.1), (planes - SHIFT - 1, planes - SHIFT + 1, -0.1)):
            slope = 0.1 + sign * flow[0, p, here]
            for f in range(FIELDS):
                out[f, p, here] = out[f, p, here] + slope * held[f, j, body]

    def step(p, carry):
        for b in range(height // 8):
            cells(rows, p, b, numbers, held, flow, gap, out)
        return carry

    lax.fori_loop(planes - SHIFT, planes, step, 0)


def add_rows(rows, f, p, sides, flow, one, two, i, out):
    tiles = one.shape[1]
    even, low, high = sides
    for y, keep, sign, value in (
        (rows - 1, high, -1.0, jnp.where(even, one[i], two[i])),
        (0, low, 1.0, jnp.where(even, two[i], one[i])),
    ):
        where = pl.ds(y, tiles, stride=rows)
        slope = keep + (sign * keep) * flow[1, p, where, :]
        out[f, p, where, :] = out[f, p, where, :] + slope * value


def sides_of():
    place = lax.axis_index("xs")
    low = jnp.where(place > 0, 0.1, 0.0)
    high = jnp.where(place < lax.axis_size("xs") - 1, 0.1, 0.0)
    return lax.rem(place, 2) == 0, low, high


def glow_kernel(rows, scale, part_in, flow, gap, e1, o1, e2, o2, part, *rest):
    *outs, picture = rest
    planes, height = part.shape[1:3]
    sides = sides_of()
    first, middle, _, _ = rows_sent(planes)
    for listed, one, two in ((first[: 2 * (planes - SHIFT)], e1, o1), (middle, e2, o2)):
        for i, (f, p) in enumerate(listed):
            add_rows(rows, f, p, sides, flow, one, two, i, part)
    for b in range(height // 8):
        here = pl.ds(8 * b, 8)
        total = jnp.zeros((8, LANES), jnp.float32)
        for p in range(planes):
            gas = (1 - gap[p, here]).astype(jnp.float32)
            total += gas * part[GLOW, p, here] * part[SPECIES, p, here]
        picture[here, :] = total * scale
    split_rows(picture, outs, height, lax.axis_size("ax") // 2)


def error_kernel(kept, got, viewer, out, stage, sem):
    stage[...] = kept[...] + got[...] - viewer[...]
    copy = pltpu.make_async_copy(stage, out, sem)
    copy.start()
    copy.wait()


def store_kernel(rows, last, part_in, flow, one, two, *rest):
    part, final, thermal, sems = rest[-4:]
    planes, _ = part.shape[1:3]
    sides = sides_of()
    ready = planes - SHIFT
    now, _, late, late_ends = rows_sent(planes)
    listed = late + late_ends if last else now
    ends, most, everything = pl.ds(ready, SHIFT), pl.ds(0, ready), pl.ds(0, planes)
    if last:
        done = [(f, everything) for f in ORDER[EARLY:]] + [(f, ends) for f in ORDER[2:EARLY]]
    else:
        done = [(f, everything) for f in ORDER[:2]] + [(f, most) for f in ORDER[2:EARLY]]
    copies = []
    for n, (f, span) in enumerate(done):
        for i, (field, p) in enumerate(listed):
            if field == f and f not in ORDER[:2]:
                add_rows(rows, f, p, sides, flow, one, two, i, part)
        target = thermal if f == SPECIES else final.at[f]
        copies.append(pltpu.make_async_copy(part.at[f, span], target.at[span], sems.at[n]))
        copies[-1].start()
    for copy in copies:
        copy.wait()


def split_rows(picture, outs, height, stage):
    if len(outs) == 1:
        outs[0][...] = picture[...]
        return
    half = height // 2
    upper = lax.rem(lax.axis_index("ax") // stage, 2)
    for keep, out in zip((upper, 1 - upper), outs):
        out[...] = picture[pl.ds(pl.multiple_of(keep * half, 8), half), :]


def join_kernel(stage, kept, got, *rest):
    *outs, picture = rest
    picture[...] = kept[...] + got[...]
    split_rows(picture, outs, picture.shape[0], stage)


def call(kernel, args, outs, scratch=(), aliases=None, us=1):
    spaces = {"v": pltpu.VMEM, "h": pltpu.HBM}
    return pl.pallas_call(
        kernel,
        out_shape=tuple(spaces[m](shape, jnp.float32) if m != "g" else jax.ShapeDtypeStruct(shape, jnp.int32) for shape, m in outs),
        in_specs=[pl.BlockSpec(memory_space=spaces[m]) for _, m in args],
        out_specs=tuple(pl.BlockSpec(memory_space=spaces.get(m, pltpu.VMEM)) for _, m in outs),
        scratch_shapes=list(scratch),
        input_output_aliases=aliases or {},
        cost_estimate=pl.CostEstimate(flops=int(us * FLOPS), bytes_accessed=0, transcendentals=0),
        compiler_params=pltpu.CompilerParams(vmem_limit_bytes=GRANT),
    )(*(pltpu.with_memory_space_constraint(a, spaces[m]) for a, m in args))


def per_device(c, t, flow, gap, owner, rate, threshold, matrix, release, viewer):
    rows = t.shape[1]
    c, t, flow, gap = (tiled(x) for x in (c, t, flow, gap))
    planes, height, _ = t.shape
    tiles = height // rows
    count = lax.axis_size("ax")
    first, middle, last, last_late = rows_sent(planes)
    first, middle, last = (
        ((len(x), tiles, LANES), "v") for x in (first, middle, last + last_late)
    )
    ends = ((FIELDS, SHIFT + 1, height, LANES), "v")
    whole = ((FIELDS, planes, height, LANES), "v")
    padded = ((FIELDS, planes + 2, height + 16, LANES), "v")
    numbers = [(x, "h") for x in (rate, threshold, matrix, release)]
    number_slots = [pltpu.SMEM(x.shape, x.dtype) for x, _ in numbers]
    sems = pltpu.SemaphoreType.DMA
    bind = functools.partial

    to_even, to_odd, old, shares = call(
        bind(send_kernel, rows), [(c, "h"), (t, "h"), (owner, "h")],
        [first, first, whole, ((planes + 2, SHIFT + 1, 8, LANES), "v")],
        [pltpu.SMEM(owner.shape, owner.dtype), sems((FIELDS + 1,))],
    )
    last_even, last_odd, lips, up, down, old = call(
        bind(more_kernel, rows), [(c, "h"), (t, "h"), (shares, "v"), (old, "v")],
        [last, last, ((FIELDS * SHIFT * 2, tiles, LANES), "v"), ends,
         ((FIELDS, height, LANES), "v"), whole],
        [sems((FIELDS,))], {3: 5},
    )
    tiling = lax.axis_size("xs")
    xs_even, xs_odd = swaps(count, tiling, 0), swaps(count, tiling, 1)
    lips = lax.ppermute(lips, "ax", ring(count, -1))
    upper = lax.ppermute(up, "ax", ring(count, -1))
    e1 = lax.ppermute(to_even, ("ax", "xs"), xs_even)
    o1 = lax.ppermute(to_odd, ("ax", "xs"), xs_odd)
    lower = lax.ppermute(down, "ax", ring(count, 1))
    held, part, flow_v, gap_v = call(
        bind(inner_kernel, rows),
        [(shares, "v"), (old, "v"), (flow, "h"), (gap, "h")] + numbers,
        [padded, whole, (flow.shape, "v"), (gap.shape, "g")],
        number_slots + [sems((6,))], us=4,
    )
    late_even, late_odd, last_even, last_odd = call(
        bind(late_kernel, rows),
        [(shares, "v"), (old, "v"), (lips, "v"), (last_even, "v"), (last_odd, "v")],
        [middle, middle, last, last], (), {3: 2, 4: 3},
    )
    e2 = lax.ppermute(late_even, ("ax", "xs"), xs_even)
    o2 = lax.ppermute(late_odd, ("ax", "xs"), xs_odd)
    e3 = lax.ppermute(last_even, ("ax", "xs"), xs_even)
    o3 = lax.ppermute(last_odd, ("ax", "xs"), xs_odd)
    held, part = call(
        bind(outer_kernel, rows),
        [(shares, "v"), (old, "v"), (upper, "v"), (lower, "v"), (held, "v"), (part, "v"),
         (flow_v, "v"), (gap_v, "v")] + numbers,
        [padded, whole], number_slots + [sems((4,))], {4: 0, 5: 1}, us=2,
    )
    final_shape = (SPECIES, planes, height, LANES)
    thermal_shape = (planes, height, LANES)
    direct = count & (count - 1) == 0 and tiles % count == 0
    pieces = 2 if direct else 1
    part, *glows = call(
        bind(glow_kernel, rows, 1.0 / owner.shape[0]),
        [(part, "v"), (flow_v, "v"), (gap_v, "v"), (e1, "v"), (o1, "v"), (e2, "v"), (o2, "v")],
        [whole] + [((height // pieces, LANES), "v")] * pieces,
        [pltpu.VMEM((height, LANES), jnp.float32)], {0: 0},
    )
    stores = [whole, (final_shape, "h"), (thermal_shape, "h")]
    part, final, thermal = call(
        bind(store_kernel, rows, False),
        [(part, "v"), (flow_v, "v"), (e1, "v"), (o1, "v")],
        stores, [sems((FIELDS,))], {0: 0},
    )
    part, final, thermal = call(
        bind(store_kernel, rows, True),
        [(part, "v"), (flow_v, "v"), (e3, "v"), (o3, "v"), (final, "h"), (thermal, "h")],
        stores, [sems((FIELDS,))], {0: 0, 4: 1, 5: 2},
    )
    place = lax.axis_index("ax")
    if direct:
        stage = count // 2
        while True:
            pairs = [(i, i ^ stage) for i in range(count)]
            kept, got = glows[0], lax.ppermute(glows[1], "ax", pairs)
            if stage == 1:
                break
            stage //= 2
            size = kept.shape[0]
            glows = call(
                bind(join_kernel, stage), [(kept, "v"), (got, "v")],
                [((size // 2, LANES), "v")] * 2, [pltpu.VMEM((size, LANES), jnp.float32)],
            )
        (error,) = call(
            error_kernel, [(kept, "v"), (got, "v"), (tiled(viewer), "v")],
            [(kept.shape, "h")], [pltpu.VMEM(kept.shape, jnp.float32), sems],
        )
        error = untiled(error, rows)
    else:
        picture = lax.psum(untiled(glows[0], rows), "ax")
        columns = picture.shape[1] // count
        mine = lax.dynamic_slice_in_dim(picture, place * columns, columns, 1)
        error = mine - viewer
    return untiled(final, rows), untiled(thermal, rows), error


def solution(mesh):
    volume, field = P(None, "ax", "xs", None), P("ax", "xs", None)
    in_specs = (volume, field, volume, field, P(), P(), P(), P(), P(), P("xs", "ax"))
    return jax.shard_map(
        per_device,
        mesh=mesh,
        in_specs=in_specs,
        out_specs=(volume, field, P("xs", "ax")),
        check_vma=False,
    )
```

time: 33.9 us -> 46.6 us (1.37)
  the two profiles are of different devices: /device:TPU:0 before, /device:TPU:13 now
where the time goes in v1:
time: 46.6 us; the launch traced here: 46.4 us
  waiting for transfers between devices  21.1 us (45%)
  starting transfers between devices  13.5 us (29%)
  Pallas kernels  11.1 us (24%)
  between operations  0.72 us (2%)
    pallas_call x10, Pallas kernels, call(): pl.pallas_call(kernel, out_shape=tuple((spaces[m](shape, jnp.float32) if...  11.1 us
    ppermute x1, waiting for transfers between devices, per_device(): e2 = lax.ppermute(late_even, ('ax', 'xs'), xs_even)  10.6 us
    ppermute x1, waiting for transfers between devices, per_device(): lips = lax.ppermute(lips, 'ax', ring(count, -1))  9.38 us
    ppermute x2, starting transfers between devices, per_device(): kept, got = (glows[0], lax.ppermute(glows[1], 'ax', pairs))  4.6 us
    ppermute x1, starting transfers between devices, per_device(): o3 = lax.ppermute(last_odd, ('ax', 'xs'), xs_odd)  2.26 us
    ppermute x1, starting transfers between devices, per_device(): e1 = lax.ppermute(to_even, ('ax', 'xs'), xs_even)  1.46 us
    ppermute x1, starting transfers between devices, per_device(): o1 = lax.ppermute(to_odd, ('ax', 'xs'), xs_odd)  1.24 us
    ppermute x1, starting transfers between devices, per_device(): o2 = lax.ppermute(late_odd, ('ax', 'xs'), xs_odd)  1.19 us
  transfers between devices with their start and end apart: 11, of which 4 were waited for; matrix products, arithmetic and copies ran while one was open for 0% of the time, Pallas kernels for 17%

profile of v1, /device:TPU:13, one launch (start us, length us, event | category | flops | bytes accessed | tf_op | source)
XLA Modules:
  0.0 46.4 jit_solution(926308008919925489)
XLA Ops:
  0.6 1.4 %shard_map.121 = (f32[50,8,128]{2,1,0:T(8,128)S(1)}, f32[50,8,128]{2,1,0:T(8,128)S(1)}, f32[10,12,32,128]{3,2,1,0:T(8,128)S(1)}, f32[14,3,8,128]{3,2,1,0:T(8,128)S(1)}) custom-call(f32[9,12,32,128]{3,2,1,0:T(8,128)} %bitcast.41, f32[12,32,128]{2,1,0:T(8,128)} %bitcast.44, s32[48]{0:T(128)} %owner.1), custom_call_target="tpu_custom_call" | custom-call | flops 100000000 | tf_op jit(solution)/shard_map/pallas_call | solution.py:388
  2.0 1.4 %shard_map.122 = (f32[66,8,128]{2,1,0:T(8,128)S(1)}, f32[66,8,128]{2,1,0:T(8,128)S(1)}, f32[40,8,128]{2,1,0:T(8,128)S(1)}, f32[10,3,32,128]{3,2,1,0:T(8,128)S(1)...) custom-call(f32[9,12,32,128]{3,2,1,0:T(8,128)} %bitcast.42, ...), custom_call_target="tpu_custom_call", output_to_operand_aliasing={{5}: (3, {})} | custom-call | flops 100000000 | tf_op jit(solution)/shard_map/pallas_call | solution.py:388
  3.4 0.7 %collective-permute-start = (f32[10,3,32,128]{3,2,1,0:T(8,128)S(1)}, f32[10,3,32,128]{3,2,1,0:T(8,128)S(1)}, u32[]{:S(2)}, u32[]{:S(2)}) collective-permute-start(f32[10,3,32,128]{3,2,1,0:T(8,128)S(1)} %get-tuple-element.35), channel_id=1, source_target_pairs={{0,24},{8,0},{16,8},{24,16},{1,25},{9,1},{17,9},{25,17},{2,26},{10... | collective-permute-start | bytes 1474568 | tf_op jit(solution)/shard_map/ppermute | solution.py:432
  4.2 0.9 %collective-permute-start.4 = (f32[40,8,128]{2,1,0:T(8,128)S(1)}, f32[40,8,128]{2,1,0:T(8,128)S(1)}, u32[]{:S(2)}, u32[]{:S(2)}) collective-permute-start(f32[40,8,128]{2,1,0:T(8,128)S(1)} %get-tuple-element.44), channel_id=1, source_target_pairs={{0,24},{8,0},{16,8},{24,16},{1,25},{9,1},{17,9},{25,17},{2,26},{10... | collective-permute-start | bytes 491528 | tf_op jit(solution)/shard_map/ppermute | solution.py:431
  5.1 0.8 %collective-permute-start.1 = (f32[10,32,128]{2,1,0:T(8,128)S(1)}, f32[10,32,128]{2,1,0:T(8,128)S(1)}, u32[]{:S(2)}, u32[]{:S(2)}) collective-permute-start(f32[10,32,128]{2,1,0:T(8,128)S(1)} %get-tuple-element.36), channel_id=1, source_target_pairs={{0,8},{8,16},{16,24},{24,0},{1,9},{9,17},{17,25},{25,1},{2,10},{10... | collective-permute-start | bytes 491528 | tf_op jit(solution)/shard_map/ppermute | solution.py:435
  5.9 9.4 %collective-permute-done.4.lips = f32[40,8,128]{2,1,0:T(8,128)S(1)} collective-permute-done((f32[40,8,128]{2,1,0:T(8,128)S(1)}, f32[40,8,128]{2,1,0:T(8,128)S(1)}, u32[]{:S(2)}, u32[]{:S(2)}) %collective-permute-start.4) | collective-permute-done | bytes 163872 | tf_op jit(solution)/shard_map/ppermute | solution.py:431
  15.3 0.3 collective-permute-start.7
  15.6 2.3 %collective-permute-start.8 = (f32[66,8,128]{2,1,0:T(8,128)S(1)}, f32[66,8,128]{2,1,0:T(8,128)S(1)}, u32[]{:S(2)}, u32[]{:S(2)}) collective-permute-start(f32[66,8,128]{2,1,0:T(8,128)S(1)} %get-tuple-element.52), channel_id=1, source_target_pairs={{1,2},{2,1},{3,4},{4,3},{5,6},{6,5},{0,8},{7,15},{9,10},{10,9},{11... | collective-permute-start | bytes 811016 | tf_op jit(solution)/shard_map/ppermute | solution.py:450
  17.9 0.0 collective-permute-start.5
  17.9 0.0 collective-permute-done.1.lower
  17.9 1.5 %collective-permute-start.2 = (f32[50,8,128]{2,1,0:T(8,128)S(1)}, f32[50,8,128]{2,1,0:T(8,128)S(1)}, u32[]{:S(2)}, u32[]{:S(2)}) collective-permute-start(f32[50,8,128]{2,1,0:T(8,128)S(1)} %get-tuple-element.42), channel_id=1, source_target_pairs={{0,1},{1,0},{2,3},{3,2},{4,5},{5,4},{6,7},{7,6},{8,9},{9,8},{10,11... | collective-permute-start | bytes 614408 | tf_op jit(solution)/shard_map/ppermute | solution.py:433
  19.3 10.6 %collective-permute-done.5.e2 = f32[4,8,128]{2,1,0:T(8,128)S(1)} collective-permute-done((f32[4,8,128]{2,1,0:T(8,128)S(1)}, f32[4,8,128]{2,1,0:T(8,128)S(1)}, u32[]{:S(2)}, u32[]{:S(2)}) %collective-permute-start.5) | collective-permute-done | bytes 16416 | tf_op jit(solution)/shard_map/ppermute | solution.py:447
  29.9 1.2 %collective-permute-start.3 = (f32[50,8,128]{2,1,0:T(8,128)S(1)}, f32[50,8,128]{2,1,0:T(8,128)S(1)}, u32[]{:S(2)}, u32[]{:S(2)}) collective-permute-start(f32[50,8,128]{2,1,0:T(8,128)S(1)} %get-tuple-element.43), channel_id=1, source_target_pairs={{1,2},{2,1},{3,4},{4,3},{5,6},{6,5},{0,8},{7,15},{9,10},{10,9},{11... | collective-permute-start | bytes 614408 | tf_op jit(solution)/shard_map/ppermute | solution.py:434
  31.1 4.1 %shard_map.123 = (f32[10,14,48,128]{3,2,1,0:T(8,128)S(1)}, f32[10,12,32,128]{3,2,1,0:T(8,128)S(1)}, f32[3,12,32,128]{3,2,1,0:T(8,128)S(1)}, s32[12,32,128]{2,1,0:T(8,128)S(1)}) custom-call(f32[14,3,8,128]{3,2,1,0:T(8,128)S(1)} %get-tuple-element.32.shares, f32[10,12,32,128]{3,2,1,0:T(8,128)S(1)} %get-tuple-element.34.old, f32[3,12,32,128]{3,2,1,0:T(8,128)} %bitcast.46, ...), custom_call_target="tpu_custom_call" | custom-call | flops 400000000 | tf_op jit(solution)/shard_map/pallas_call | solution.py:388
  35.2 0.0 collective-permute-done.upper
  35.2 1.2 %collective-permute-start.6 = (f32[4,8,128]{2,1,0:T(8,128)S(1)}, f32[4,8,128]{2,1,0:T(8,128)S(1)}, u32[]{:S(2)}, u32[]{:S(2)}) collective-permute-start(f32[4,8,128]{2,1,0:T(8,128)S(1)} %get-tuple-element.48), channel_id=1, source_target_pairs={{1,2},{2,1},{3,4},{4,3},{5,6},{6,5},{0,8},{7,15},{9,10},{10,9},{11... | collective-permute-start | bytes 49160 | tf_op jit(solution)/shard_map/ppermute | solution.py:448
  36.4 1.4 %shard_map.124 = (f32[10,14,48,128]{3,2,1,0:T(8,128)S(1)}, f32[10,12,32,128]{3,2,1,0:T(8,128)S(1)}) custom-call(f32[14,3,8,128]{3,2,1,0:T(8,128)S(1)} %get-tuple-element.32.shares, f32[10,12,32,128]{3,2,1,0:T(8,128)S(1)} %get-tuple-element.34.old, f32[10,3,32,128]{3,2,1,0:T(8,128)S(1)} %collective-permute-done.upper, ...), custom_call_target="tpu_custom_call", output_to_operand_aliasing={{0}: (4, {}), {1}: (5, {})} | custom-call | flops 200000000 | tf_op jit(solution)/shard_map/pallas_call | solution.py:388
  37.9 0.9 %collective-permute-done.6.o2 = f32[4,8,128]{2,1,0:T(8,128)S(1)} collective-permute-done((f32[4,8,128]{2,1,0:T(8,128)S(1)}, f32[4,8,128]{2,1,0:T(8,128)S(1)}, u32[]{:S(2)}, u32[]{:S(2)}) %collective-permute-start.6) | collective-permute-done | bytes 16416 | tf_op jit(solution)/shard_map/ppermute | solution.py:448
  38.8 0.0 collective-permute-done.2.e1.one
  38.8 0.0 collective-permute-done.3.o1.two
  38.8 0.1 shard_map.126
  38.9 1.4 %collective-permute-start.9 = (f32[16,128]{1,0:T(8,128)S(1)}, f32[16,128]{1,0:T(8,128)S(1)}, u32[]{:S(2)}, u32[]{:S(2)}) collective-permute-start(f32[16,128]{1,0:T(8,128)S(1)} %get-tuple-element.58), channel_id=1, source_target_pairs={{0,16},{8,24},{16,0},{24,8},{1,17},{9,25},{17,1},{25,9},{2,18},{10... | collective-permute-start | bytes 24584 | tf_op jit(solution)/shard_map/ppermute | solution.py:483
  40.3 1.0 %shard_map.127 = (f32[10,12,32,128]{3,2,1,0:T(8,128)S(1)}, f32[9,12,32,128]{3,2,1,0:T(8,128)}, f32[12,32,128]{2,1,0:T(8,128)}) custom-call(f32[10,12,32,128]{3,2,1,0:T(8,128)S(1)} %get-tuple-element.49.part_in, f32[3,12,32,128]{3,2,1,0:T(8,128)S(1)} %get-tuple-element.39.flow, ...), custom_call_target="tpu_custom_call", output_to_operand_aliasing={{0}: (0, {})} | custom-call | flops 100000000 | tf_op jit(solution)/shard_map/pallas_call | solution.py:388
  41.3 0.2 collective-permute-done.9.got
  41.5 3.2 %collective-permute-start.10 = (f32[8,128]{1,0:T(8,128)S(1)}, f32[8,128]{1,0:T(8,128)S(1)}, u32[]{:S(2)}, u32[]{:S(2)}) collective-permute-start(f32[8,128]{1,0:T(8,128)S(1)} %get-tuple-element.60), channel_id=1, source_target_pairs={{0,8},{8,0},{16,24},{24,16},{1,9},{9,1},{17,25},{25,17},{2,10},{10... | collective-permute-start | bytes 12296 | tf_op jit(solution)/shard_map/ppermute | solution.py:483
  44.7 0.0 collective-permute-done.7.one
  44.7 0.0 collective-permute-done.8.two
  44.7 0.0 copy-start
  44.7 1.1 %shard_map.128 = (f32[10,12,32,128]{3,2,1,0:T(8,128)S(1)}, f32[9,12,32,128]{3,2,1,0:T(8,128)}, f32[12,32,128]{2,1,0:T(8,128)}) custom-call(f32[10,12,32,128]{3,2,1,0:T(8,128)S(1)} %get-tuple-element.50.part_in, f32[3,12,32,128]{3,2,1,0:T(8,128)S(1)} %get-tuple-element.39.flow, ...), custom_call_target="tpu_custom_call", output_to_operand_aliasing={{0}: (0, {}), {1}: (4, {}), {2}: (5, {})} | custom-call | flops 100000000 | tf_op jit(solution)/shard_map/pallas_call | solution.py:388
  45.8 0.0 collective-permute-done.10.got
  45.8 0.0 copy-done
  45.8 0.6 %shard_map.130 = f32[8,128]{1,0:T(8,128)} custom-call(f32[8,128]{1,0:T(8,128)S(1)} %get-tuple-element.59.kept, f32[8,128]{1,0:T(8,128)S(1)} %collective-permute-done.10.got, f32[8,128]{1,0:T(8,128)S(1)} %bitcast.40), custom_call_target="tpu_custom_call" | custom-call | flops 100000000 | tf_op jit(solution)/shard_map/pallas_call | solution.py:388
  (2 shorter events, 0.0 us)
Async XLA Ops:
  3.4 31.8 %collective-permute-start = (f32[10,3,32,128]{3,2,1,0:T(8,128)S(1)}, f32[10,3,32,128]{3,2,1,0:T(8,128)S(1)}, u32[]{:S(2)}, u32[]{:S(2)}) collective-permute-start(f32[10,3,32,128]{3,2,1,0:T(8,128)S(1)} %get-tuple-element.35), channel_id=1, source_target_pairs={{0,24},{8,0},{16,8},{24,16},{1,25},{9,1},{17,9},{25,17},{2,26},{10... | collective-permute-start | bytes 1474568 | tf_op jit(solution)/shard_map/ppermute | solution.py:432
  4.2 11.1 %collective-permute-start.4 = (f32[40,8,128]{2,1,0:T(8,128)S(1)}, f32[40,8,128]{2,1,0:T(8,128)S(1)}, u32[]{:S(2)}, u32[]{:S(2)}) collective-permute-start(f32[40,8,128]{2,1,0:T(8,128)S(1)} %get-tuple-element.44), channel_id=1, source_target_pairs={{0,24},{8,0},{16,8},{24,16},{1,25},{9,1},{17,9},{25,17},{2,26},{10... | collective-permute-start | bytes 491528 | tf_op jit(solution)/shard_map/ppermute | solution.py:431
  5.1 12.8 %collective-permute-start.1 = (f32[10,32,128]{2,1,0:T(8,128)S(1)}, f32[10,32,128]{2,1,0:T(8,128)S(1)}, u32[]{:S(2)}, u32[]{:S(2)}) collective-permute-start(f32[10,32,128]{2,1,0:T(8,128)S(1)} %get-tuple-element.36), channel_id=1, source_target_pairs={{0,8},{8,16},{16,24},{24,0},{1,9},{9,17},{17,25},{25,1},{2,10},{10... | collective-permute-start | bytes 491528 | tf_op jit(solution)/shard_map/ppermute | solution.py:435
  15.3 29.4 %collective-permute-start.7 = (f32[66,8,128]{2,1,0:T(8,128)S(1)}, f32[66,8,128]{2,1,0:T(8,128)S(1)}, u32[]{:S(2)}, u32[]{:S(2)}) collective-permute-start(f32[66,8,128]{2,1,0:T(8,128)S(1)} %get-tuple-element.51), channel_id=1, source_target_pairs={{0,1},{1,0},{2,3},{3,2},{4,5},{5,4},{6,7},{7,6},{8,9},{9,8},{10,11... | collective-permute-start | bytes 811016 | tf_op jit(solution)/shard_map/ppermute | solution.py:449
  15.6 29.1 %collective-permute-start.8 = (f32[66,8,128]{2,1,0:T(8,128)S(1)}, f32[66,8,128]{2,1,0:T(8,128)S(1)}, u32[]{:S(2)}, u32[]{:S(2)}) collective-permute-start(f32[66,8,128]{2,1,0:T(8,128)S(1)} %get-tuple-element.52), channel_id=1, source_target_pairs={{1,2},{2,1},{3,4},{4,3},{5,6},{6,5},{0,8},{7,15},{9,10},{10,9},{11... | collective-permute-start | bytes 811016 | tf_op jit(solution)/shard_map/ppermute | solution.py:450
  17.9 12.0 %collective-permute-start.5 = (f32[4,8,128]{2,1,0:T(8,128)S(1)}, f32[4,8,128]{2,1,0:T(8,128)S(1)}, u32[]{:S(2)}, u32[]{:S(2)}) collective-permute-start(f32[4,8,128]{2,1,0:T(8,128)S(1)} %get-tuple-element.47), channel_id=1, source_target_pairs={{0,1},{1,0},{2,3},{3,2},{4,5},{5,4},{6,7},{7,6},{8,9},{9,8},{10,11... | collective-permute-start | bytes 49160 | tf_op jit(solution)/shard_map/ppermute | solution.py:447
  17.9 20.9 %collective-permute-start.2 = (f32[50,8,128]{2,1,0:T(8,128)S(1)}, f32[50,8,128]{2,1,0:T(8,128)S(1)}, u32[]{:S(2)}, u32[]{:S(2)}) collective-permute-start(f32[50,8,128]{2,1,0:T(8,128)S(1)} %get-tuple-element.42), channel_id=1, source_target_pairs={{0,1},{1,0},{2,3},{3,2},{4,5},{5,4},{6,7},{7,6},{8,9},{9,8},{10,11... | collective-permute-start | bytes 614408 | tf_op jit(solution)/shard_map/ppermute | solution.py:433
  29.9 8.9 %collective-permute-start.3 = (f32[50,8,128]{2,1,0:T(8,128)S(1)}, f32[50,8,128]{2,1,0:T(8,128)S(1)}, u32[]{:S(2)}, u32[]{:S(2)}) collective-permute-start(f32[50,8,128]{2,1,0:T(8,128)S(1)} %get-tuple-element.43), channel_id=1, source_target_pairs={{1,2},{2,1},{3,4},{4,3},{5,6},{6,5},{0,8},{7,15},{9,10},{10,9},{11... | collective-permute-start | bytes 614408 | tf_op jit(solution)/shard_map/ppermute | solution.py:434
  35.2 3.6 %collective-permute-start.6 = (f32[4,8,128]{2,1,0:T(8,128)S(1)}, f32[4,8,128]{2,1,0:T(8,128)S(1)}, u32[]{:S(2)}, u32[]{:S(2)}) collective-permute-start(f32[4,8,128]{2,1,0:T(8,128)S(1)} %get-tuple-element.48), channel_id=1, source_target_pairs={{1,2},{2,1},{3,4},{4,3},{5,6},{6,5},{0,8},{7,15},{9,10},{10,9},{11... | collective-permute-start | bytes 49160 | tf_op jit(solution)/shard_map/ppermute | solution.py:448
  38.9 2.6 %collective-permute-start.9 = (f32[16,128]{1,0:T(8,128)S(1)}, f32[16,128]{1,0:T(8,128)S(1)}, u32[]{:S(2)}, u32[]{:S(2)}) collective-permute-start(f32[16,128]{1,0:T(8,128)S(1)} %get-tuple-element.58), channel_id=1, source_target_pairs={{0,16},{8,24},{16,0},{24,8},{1,17},{9,25},{17,1},{25,9},{2,18},{10... | collective-permute-start | bytes 24584 | tf_op jit(solution)/shard_map/ppermute | solution.py:483
  41.5 4.3 %collective-permute-start.10 = (f32[8,128]{1,0:T(8,128)S(1)}, f32[8,128]{1,0:T(8,128)S(1)}, u32[]{:S(2)}, u32[]{:S(2)}) collective-permute-start(f32[8,128]{1,0:T(8,128)S(1)} %get-tuple-element.60), channel_id=1, source_target_pairs={{0,8},{8,0},{16,24},{24,16},{1,9},{9,1},{17,25},{25,17},{2,10},{10... | collective-permute-start | bytes 12296 | tf_op jit(solution)/shard_map/ppermute | solution.py:483
  44.7 1.1 %copy-start = (f32[4,256]{1,0:T(4,128)S(1)}, f32[4,256]{1,0:T(4,128)}, u32[]{:S(2)}) copy-start(f32[4,256]{1,0:T(4,128)} %param.19) | copy-start | bytes 12292

commit v2 on v1

--- a/solution.py
+++ b/solution.py
@@ -12,7 +12,8 @@
 FIELDS = SPECIES + 1
 GLOW = 4
 ORDER = (GLOW, SPECIES) + tuple(f for f in range(SPECIES) if f != GLOW)
-EARLY = 5
+EARLY = 6
+HEAD = 4
 SHIFT = 2
 LANES = 128
 GRANT = 16 << 20
@@ -52,18 +53,22 @@
     return [(i, (i + distance) % count) for i in range(count)]
 
 
-def remap_weights(owner, plane):
+def remap_weights(owner, first, count):
     total = owner.shape[0]
-    inside = jnp.logical_and(plane >= 0, plane < total)
-    hits = []
-    for k in range(SHIFT + 1):
-        p = plane + k
-        mine = owner[jnp.clip(p, 0, total - 1)] == plane
-        hits.append(jnp.where(inside & (p < total) & mine, 1.0, 0.0))
-    count = hits[0] + hits[1] + hits[2]
-    share = jnp.where(count > 2.5, 1.0 / 3.0, jnp.where(count > 1.5, 0.5, 1.0))
-    kept = jnp.where(jnp.logical_and(inside, count < 0.5), 1.0, 0.0)
-    return hits[0] * share + kept, hits[1] * share, hits[2] * share
+    landed = []
+    for p in range(count + SHIFT):
+        there = owner[jnp.clip(first + p, 0, total - 1)]
+        landed.append(jnp.where(first + p < total, there, -1))
+    result = []
+    for j in range(count):
+        plane = first + j
+        hits = [landed[j + k] == plane for k in range(SHIFT + 1)]
+        number = sum(jnp.where(hit, 1, 0) for hit in hits)
+        share = jnp.where(number == 3, 1.0 / 3.0, jnp.where(number == 2, 0.5, 1.0))
+        share = jnp.where(jnp.logical_and(plane >= 0, plane < total), share, 0.0)
+        hits[0] = jnp.logical_or(hits[0], number == 0)
+        result.append([jnp.where(hit, share, 0.0) for hit in hits])
+    return result
 
 
 def mix(weights, values):
@@ -97,43 +102,56 @@
     return copies
 
 
-def edge_rows(rows, f, listed, old, weights, outs):
+def edge_rows(rows, f, start, listed, old, weights, out):
     planes, height = old.shape[1:3]
     tiles = height // rows
-    for start, out in zip(edge_starts(rows), outs):
-        edge = [old[f, p, pl.ds(start, tiles, stride=rows), :] for p in range(planes)]
-        for j in range(planes - SHIFT):
-            out[listed.index((f, j))] = mix(weights[j + 1], edge[j : j + 3])
-
-
-def send_kernel(rows, c, t, owner, to_even, to_odd, old, shares, table, sems):
+    edge = [old[f, p, pl.ds(start, tiles, stride=rows), :] for p in range(planes)]
+    for j in range(planes - SHIFT):
+        out[listed.index((f, j))] = mix(weights[j + 1], edge[j : j + 3])
+
+
+def send_kernel(rows, c, t, owner, to_even, shares, table, edge, sems):
     planes = t.shape[0]
+    tiles = t.shape[2] // LANES
     wanted = pltpu.make_async_copy(owner, table, sems.at[FIELDS])
     wanted.start()
-    copies = load_fields(c, t, ORDER[:EARLY], old, sems)
+    start = edge_starts(rows)[0]
+    copies = []
+    for i, f in enumerate(ORDER[:EARLY]):
+        source = old_field(c, t, f).at[:, pl.ds(start, 1), :]
+        copies.append(pltpu.make_async_copy(source, edge.at[i], sems.at[f]))
+        copies[-1].start()
     wanted.wait()
     first = lax.axis_index("ax") * planes
-    weights = []
-    for j in range(planes + 2):
-        weights.append(remap_weights(table, first - 1 + j))
-        for k, w in enumerate(weights[j]):
+    weights = remap_weights(table, first - 1, planes + 2)
+    for j, triple in enumerate(weights):
+        for k, w in enumerate(triple):
             shares[j, k] = jnp.full((8, LANES), w, jnp.float32)
-    for f in ORDER[:EARLY]:
-        copies[f].wait()
-        edge_rows(rows, f, rows_sent(planes)[0], old, weights, (to_even, to_odd))
+    listed = rows_sent(planes)[0]
+    for i, f in enumerate(ORDER[:EARLY]):
+        copies[i].wait()
+        for j in range(planes - SHIFT):
+            to_even[listed.index((f, j))] = mix(
+                weights[j + 1], [edge[i, j + k].reshape(tiles, LANES) for k in range(SHIFT + 1)]
+            )
 
 
 def more_kernel(
-    rows, c, t, shares, old_in, last_even, last_odd, lips, up, down, old, sems,
+    rows, c, t, shares, to_odd, last_even, last_odd, lips, up, down, old, sems,
 ):
     planes, height, _ = t.shape
     tiles = height // rows
-    copies = load_fields(c, t, ORDER[EARLY:], old, sems)
+    copies = load_fields(c, t, ORDER, old, sems)
     weights = [[shares[j, k, :tiles] for k in range(SHIFT + 1)] for j in range(planes + 2)]
+    even_start, odd_start = edge_starts(rows)
+    first, _, last, _ = rows_sent(planes)
     for f in ORDER:
-        if f in copies:
-            copies[f].wait()
-            edge_rows(rows, f, rows_sent(planes)[2], old, weights, (last_even, last_odd))
+        copies[f].wait()
+        if f in ORDER[EARLY:]:
+            edge_rows(rows, f, even_start, last, old, weights, last_even)
+            edge_rows(rows, f, odd_start, last, old, weights, last_odd)
+        else:
+            edge_rows(rows, f, odd_start, first, old, weights, to_odd)
         up[f] = old[f, 0 : SHIFT + 1]
         for p in range(SHIFT):
             for i, y in enumerate((0, rows - 1)):
@@ -251,7 +269,24 @@
             cells(rows, p, b, numbers, held, flow, gap, out)
         return carry
 
-    lax.fori_loop(0, planes - SHIFT, step, 0)
+    lax.fori_loop(0, HEAD, step, 0)
+
+
+def middle_kernel(
+    rows, held, out_in, flow, gap, rate, threshold, matrix, release, out, s_rate, s_threshold,
+    s_matrix, s_release, sems,
+):
+    planes, height = out.shape[1:3]
+    numbers = (s_rate, s_threshold, s_matrix, s_release)
+    for copy in fetch((rate, threshold, matrix, release), numbers, sems):
+        copy.wait()
+
+    def step(p, carry):
+        for b in range(height // 8):
+            cells(rows, p, b, numbers, held, flow, gap, out)
+        return carry
+
+    lax.fori_loop(HEAD, planes - SHIFT, step, 0)
 
 
 def outer_kernel(
@@ -399,6 +434,7 @@
 
 def per_device(c, t, flow, gap, owner, rate, threshold, matrix, release, viewer):
     rows = t.shape[1]
+    c_rows, t_rows = c, t
     c, t, flow, gap = (tiled(x) for x in (c, t, flow, gap))
     planes, height, _ = t.shape
     tiles = height // rows
@@ -415,16 +451,17 @@
     sems = pltpu.SemaphoreType.DMA
     bind = functools.partial
 
-    to_even, to_odd, old, shares = call(
-        bind(send_kernel, rows), [(c, "h"), (t, "h"), (owner, "h")],
-        [first, first, whole, ((planes + 2, SHIFT + 1, 8, LANES), "v")],
-        [pltpu.SMEM(owner.shape, owner.dtype), sems((FIELDS + 1,))],
-    )
-    last_even, last_odd, lips, up, down, old = call(
-        bind(more_kernel, rows), [(c, "h"), (t, "h"), (shares, "v"), (old, "v")],
-        [last, last, ((FIELDS * SHIFT * 2, tiles, LANES), "v"), ends,
+    to_even, shares = call(
+        bind(send_kernel, rows), [(c_rows, "h"), (t_rows, "h"), (owner, "h")],
+        [first, ((planes + 2, SHIFT + 1, 8, LANES), "v")],
+        [pltpu.SMEM(owner.shape, owner.dtype),
+         pltpu.VMEM((EARLY, planes, 1, t_rows.shape[2]), jnp.float32), sems((FIELDS + 1,))],
+    )
+    to_odd, last_even, last_odd, lips, up, down, old = call(
+        bind(more_kernel, rows), [(c, "h"), (t, "h"), (shares, "v")],
+        [first, last, last, ((FIELDS * SHIFT * 2, tiles, LANES), "v"), ends,
          ((FIELDS, height, LANES), "v"), whole],
-        [sems((FIELDS,))], {3: 5},
+        [sems((FIELDS,))],
     )
     tiling = lax.axis_size("xs")
     xs_even, xs_odd = swaps(count, tiling, 0), swaps(count, tiling, 1)
@@ -448,6 +485,11 @@
     o2 = lax.ppermute(late_odd, ("ax", "xs"), xs_odd)
     e3 = lax.ppermute(last_even, ("ax", "xs"), xs_even)
     o3 = lax.ppermute(last_odd, ("ax", "xs"), xs_odd)
+    (part,) = call(
+        bind(middle_kernel, rows),
+        [(held, "v"), (part, "v"), (flow_v, "v"), (gap_v, "v")] + numbers,
+        [whole], number_slots + [sems((4,))], {1: 0}, us=2,
+    )
     held, part = call(
         bind(outer_kernel, rows),
         [(shares, "v"), (old, "v"), (upper, "v"), (lower, "v"), (held, "v"), (part, "v"),

time: 46.6 us -> 37 us (0.79)
  the two profiles are of different devices: /device:TPU:13 before, /device:TPU:25 now
where the time goes in v2:
time: 37 us; the launch traced here: 36.7 us
  starting transfers between devices  12.8 us (35%)
  Pallas kernels  11.8 us (32%)
  waiting for transfers between devices  11.3 us (31%)
  between operations  0.74 us (2%)
    pallas_call x11, Pallas kernels, call(): pl.pallas_call(kernel, out_shape=tuple((spaces[m](shape, jnp.float32) if...  11.8 us
    ppermute x1, waiting for transfers between devices, per_device(): lips = lax.ppermute(lips, 'ax', ring(count, -1))  8.32 us
    ppermute x2, starting transfers between devices, per_device(): kept, got = (glows[0], lax.ppermute(glows[1], 'ax', pairs))  5 us
    ppermute x1, waiting for transfers between devices, per_device(): e2 = lax.ppermute(late_even, ('ax', 'xs'), xs_even)  2.02 us
    ppermute x1, starting transfers between devices, per_device(): o2 = lax.ppermute(late_odd, ('ax', 'xs'), xs_odd)  1.3 us
    ppermute x1, starting transfers between devices, per_device(): e1 = lax.ppermute(to_even, ('ax', 'xs'), xs_even)  1.24 us
    ppermute x1, starting transfers between devices, per_device(): o3 = lax.ppermute(last_odd, ('ax', 'xs'), xs_odd)  1.13 us
    ppermute x1, starting transfers between devices, per_device(): e2 = lax.ppermute(late_even, ('ax', 'xs'), xs_even)  1.01 us
  transfers between devices with their start and end apart: 11, of which 3 were waited for; matrix products, arithmetic and copies ran while one was open for 0% of the time, Pallas kernels for 23%

profile of v2, /device:TPU:25, one launch (start us, length us, event | category | flops | bytes accessed | tf_op | source)
XLA Modules:
  0.0 36.7 jit_solution(12457826760843161674)
XLA Ops:
  0.6 1.0 %shard_map.121 = (f32[60,8,128]{2,1,0:T(8,128)S(1)}, f32[14,3,8,128]{3,2,1,0:T(8,128)S(1)}) custom-call(f32[9,12,4,1024]{3,2,1,0:T(4,128)} %c.1, f32[12,4,1024]{2,1,0:T(4,128)} %t.1, s32[48]{0:T(128)} %owner.1), custom_call_target="tpu_custom_call" | custom-call | flops 100000000 | tf_op jit(solution)/shard_map/pallas_call | solution.py:423
  1.7 1.7 %shard_map.122 = (f32[60,8,128]{2,1,0:T(8,128)S(1)}, f32[56,8,128]{2,1,0:T(8,128)S(1)}, f32[56,8,128]{2,1,0:T(8,128)S(1)}, f32[40,8,128]{2,1,0:T(8,128)S(1)}, f3...) custom-call(f32[9,12,32,128]{3,2,1,0:T(8,128)} %bitcast.41, ...), custom_call_target="tpu_custom_call" | custom-call | flops 100000000 | tf_op jit(solution)/shard_map/pallas_call | solution.py:423
  3.4 0.7 %collective-permute-start = (f32[10,3,32,128]{3,2,1,0:T(8,128)S(1)}, f32[10,3,32,128]{3,2,1,0:T(8,128)S(1)}, u32[]{:S(2)}, u32[]{:S(2)}) collective-permute-start(f32[10,3,32,128]{3,2,1,0:T(8,128)S(1)} %get-tuple-element.33), channel_id=1, source_target_pairs={{0,24},{8,0},{16,8},{24,16},{1,25},{9,1},{17,9},{25,17},{2,26},{10... | collective-permute-start | bytes 1474568 | tf_op jit(solution)/shard_map/ppermute | solution.py:469
  4.1 0.9 %collective-permute-start.4 = (f32[40,8,128]{2,1,0:T(8,128)S(1)}, f32[40,8,128]{2,1,0:T(8,128)S(1)}, u32[]{:S(2)}, u32[]{:S(2)}) collective-permute-start(f32[40,8,128]{2,1,0:T(8,128)S(1)} %get-tuple-element.42), channel_id=1, source_target_pairs={{0,24},{8,0},{16,8},{24,16},{1,25},{9,1},{17,9},{25,17},{2,26},{10... | collective-permute-start | bytes 491528 | tf_op jit(solution)/shard_map/ppermute | solution.py:468
  5.0 0.8 %collective-permute-start.1 = (f32[10,32,128]{2,1,0:T(8,128)S(1)}, f32[10,32,128]{2,1,0:T(8,128)S(1)}, u32[]{:S(2)}, u32[]{:S(2)}) collective-permute-start(f32[10,32,128]{2,1,0:T(8,128)S(1)} %get-tuple-element.34), channel_id=1, source_target_pairs={{0,8},{8,16},{16,24},{24,0},{1,9},{9,17},{17,25},{25,1},{2,10},{10... | collective-permute-start | bytes 491528 | tf_op jit(solution)/shard_map/ppermute | solution.py:472
  5.8 1.2 %collective-permute-start.2 = (f32[60,8,128]{2,1,0:T(8,128)S(1)}, f32[60,8,128]{2,1,0:T(8,128)S(1)}, u32[]{:S(2)}, u32[]{:S(2)}) collective-permute-start(f32[60,8,128]{2,1,0:T(8,128)S(1)} %get-tuple-element.40), channel_id=1, source_target_pairs={{0,1},{1,0},{2,3},{3,2},{4,5},{5,4},{6,7},{7,6},{8,9},{9,8},{10,11... | collective-permute-start | bytes 737288 | tf_op jit(solution)/shard_map/ppermute | solution.py:470
  7.1 0.1 collective-permute-start.3
  7.2 8.3 %collective-permute-done.4.lips = f32[40,8,128]{2,1,0:T(8,128)S(1)} collective-permute-done((f32[40,8,128]{2,1,0:T(8,128)S(1)}, f32[40,8,128]{2,1,0:T(8,128)S(1)}, u32[]{:S(2)}, u32[]{:S(2)}) %collective-permute-start.4) | collective-permute-done | bytes 163872 | tf_op jit(solution)/shard_map/ppermute | solution.py:468
  15.6 1.0 %collective-permute-start.5 = (f32[4,8,128]{2,1,0:T(8,128)S(1)}, f32[4,8,128]{2,1,0:T(8,128)S(1)}, u32[]{:S(2)}, u32[]{:S(2)}) collective-permute-start(f32[4,8,128]{2,1,0:T(8,128)S(1)} %get-tuple-element.45), channel_id=1, source_target_pairs={{0,1},{1,0},{2,3},{3,2},{4,5},{5,4},{6,7},{7,6},{8,9},{9,8},{10,11... | collective-permute-start | bytes 49160 | tf_op jit(solution)/shard_map/ppermute | solution.py:484
  16.6 0.0 collective-permute-done.1.lower
  16.6 0.5 %collective-permute-start.7 = (f32[56,8,128]{2,1,0:T(8,128)S(1)}, f32[56,8,128]{2,1,0:T(8,128)S(1)}, u32[]{:S(2)}, u32[]{:S(2)}) collective-permute-start(f32[56,8,128]{2,1,0:T(8,128)S(1)} %get-tuple-element.49), channel_id=1, source_target_pairs={{0,1},{1,0},{2,3},{3,2},{4,5},{5,4},{6,7},{7,6},{8,9},{9,8},{10,11... | collective-permute-start | bytes 688136 | tf_op jit(solution)/shard_map/ppermute | solution.py:486
  17.1 2.0 %collective-permute-done.5.e2 = f32[4,8,128]{2,1,0:T(8,128)S(1)} collective-permute-done((f32[4,8,128]{2,1,0:T(8,128)S(1)}, f32[4,8,128]{2,1,0:T(8,128)S(1)}, u32[]{:S(2)}, u32[]{:S(2)}) %collective-permute-start.5) | collective-permute-done | bytes 16416 | tf_op jit(solution)/shard_map/ppermute | solution.py:484
  19.1 1.1 %collective-permute-start.8 = (f32[56,8,128]{2,1,0:T(8,128)S(1)}, f32[56,8,128]{2,1,0:T(8,128)S(1)}, u32[]{:S(2)}, u32[]{:S(2)}) collective-permute-start(f32[56,8,128]{2,1,0:T(8,128)S(1)} %get-tuple-element.50), channel_id=1, source_target_pairs={{1,2},{2,1},{3,4},{4,3},{5,6},{6,5},{0,8},{7,15},{9,10},{10,9},{11... | collective-permute-start | bytes 688136 | tf_op jit(solution)/shard_map/ppermute | solution.py:487
  20.2 2.3 %shard_map.123 = (f32[10,14,48,128]{3,2,1,0:T(8,128)S(1)}, f32[10,12,32,128]{3,2,1,0:T(8,128)S(1)}, f32[3,12,32,128]{3,2,1,0:T(8,128)S(1)}, s32[12,32,128]{2,1,0:T(8,128)S(1)}) custom-call(f32[14,3,8,128]{3,2,1,0:T(8,128)S(1)} %get-tuple-element.31.shares, f32[10,12,32,128]{3,2,1,0:T(8,128)S(1)} %get-tuple-element.32.old, f32[3,12,32,128]{3,2,1,0:T(8,128)} %bitcast.44, ...), custom_call_target="tpu_custom_call" | custom-call | flops 400000000 | tf_op jit(solution)/shard_map/pallas_call | solution.py:423
  22.6 2.5 %shard_map.124.out_in = f32[10,12,32,128]{3,2,1,0:T(8,128)S(1)} custom-call(f32[10,14,48,128]{3,2,1,0:T(8,128)S(1)} %get-tuple-element.35.held.held_in, f32[10,12,32,128]{3,2,1,0:T(8,128)S(1)} %get-tuple-element.36.out_in, f32[3,12,32,128]{3,2,1,0:T(8,128)S(1)} %get-tuple-element.37.flow, ...), custom_call_target="tpu_custom_call", output_to_operand_aliasing={{}: (1, {})} | custom-call | flops 200000000 | tf_op jit(solution)/shard_map/pallas_call | solution.py:423
  25.1 0.0 collective-permute-done.upper
  25.1 1.3 %collective-permute-start.6 = (f32[4,8,128]{2,1,0:T(8,128)S(1)}, f32[4,8,128]{2,1,0:T(8,128)S(1)}, u32[]{:S(2)}, u32[]{:S(2)}) collective-permute-start(f32[4,8,128]{2,1,0:T(8,128)S(1)} %get-tuple-element.46), channel_id=1, source_target_pairs={{1,2},{2,1},{3,4},{4,3},{5,6},{6,5},{0,8},{7,15},{9,10},{10,9},{11... | collective-permute-start | bytes 49160 | tf_op jit(solution)/shard_map/ppermute | solution.py:485
  26.4 1.4 %shard_map.125 = (f32[10,14,48,128]{3,2,1,0:T(8,128)S(1)}, f32[10,12,32,128]{3,2,1,0:T(8,128)S(1)}) custom-call(f32[14,3,8,128]{3,2,1,0:T(8,128)S(1)} %get-tuple-element.31.shares, f32[10,12,32,128]{3,2,1,0:T(8,128)S(1)} %get-tuple-element.32.old, f32[10,3,32,128]{3,2,1,0:T(8,128)S(1)} %collective-permute-done.upper, ...), custom_call_target="tpu_custom_call", output_to_operand_aliasing={{0}: (4, {}), {1}: (5, {})} | custom-call | flops 200000000 | tf_op jit(solution)/shard_map/pallas_call | solution.py:423
  27.9 0.9 %collective-permute-done.6.o2 = f32[4,8,128]{2,1,0:T(8,128)S(1)} collective-permute-done((f32[4,8,128]{2,1,0:T(8,128)S(1)}, f32[4,8,128]{2,1,0:T(8,128)S(1)}, u32[]{:S(2)}, u32[]{:S(2)}) %collective-permute-start.6) | collective-permute-done | bytes 16416 | tf_op jit(solution)/shard_map/ppermute | solution.py:485
  28.8 0.0 collective-permute-done.2.e1.one
  28.8 0.0 collective-permute-done.3.o1.two
  28.8 0.1 shard_map.127
  28.9 1.7 %collective-permute-start.9 = (f32[16,128]{1,0:T(8,128)S(1)}, f32[16,128]{1,0:T(8,128)S(1)}, u32[]{:S(2)}, u32[]{:S(2)}) collective-permute-start(f32[16,128]{1,0:T(8,128)S(1)} %get-tuple-element.56), channel_id=1, source_target_pairs={{0,16},{8,24},{16,0},{24,8},{1,17},{9,25},{17,1},{25,9},{2,18},{10... | collective-permute-start | bytes 24584 | tf_op jit(solution)/shard_map/ppermute | solution.py:525
  30.6 1.0 %shard_map.128 = (f32[10,12,32,128]{3,2,1,0:T(8,128)S(1)}, f32[9,12,32,128]{3,2,1,0:T(8,128)}, f32[12,32,128]{2,1,0:T(8,128)}) custom-call(f32[10,12,32,128]{3,2,1,0:T(8,128)S(1)} %get-tuple-element.47.part_in, f32[3,12,32,128]{3,2,1,0:T(8,128)S(1)} %get-tuple-element.37.flow, ...), custom_call_target="tpu_custom_call", output_to_operand_aliasing={{0}: (0, {})} | custom-call | flops 100000000 | tf_op jit(solution)/shard_map/pallas_call | solution.py:423
  31.6 0.0 collective-permute-done.9.got
  31.7 3.3 %collective-permute-start.10 = (f32[8,128]{1,0:T(8,128)S(1)}, f32[8,128]{1,0:T(8,128)S(1)}, u32[]{:S(2)}, u32[]{:S(2)}) collective-permute-start(f32[8,128]{1,0:T(8,128)S(1)} %get-tuple-element.58), channel_id=1, source_target_pairs={{0,8},{8,0},{16,24},{24,16},{1,9},{9,1},{17,25},{25,17},{2,10},{10... | collective-permute-start | bytes 12296 | tf_op jit(solution)/shard_map/ppermute | solution.py:525
  35.0 0.0 collective-permute-done.7.one
  35.0 0.0 collective-permute-done.8.two
  35.0 0.0 copy-start
  35.0 1.0 %shard_map.129 = (f32[10,12,32,128]{3,2,1,0:T(8,128)S(1)}, f32[9,12,32,128]{3,2,1,0:T(8,128)}, f32[12,32,128]{2,1,0:T(8,128)}) custom-call(f32[10,12,32,128]{3,2,1,0:T(8,128)S(1)} %get-tuple-element.48.part_in, f32[3,12,32,128]{3,2,1,0:T(8,128)S(1)} %get-tuple-element.37.flow, ...), custom_call_target="tpu_custom_call", output_to_operand_aliasing={{0}: (0, {}), {1}: (4, {}), {2}: (5, {})} | custom-call | flops 100000000 | tf_op jit(solution)/shard_map/pallas_call | solution.py:423
  36.0 0.0 collective-permute-done.10.got
  36.0 0.0 copy-done
  36.0 0.6 %shard_map.131 = f32[8,128]{1,0:T(8,128)} custom-call(f32[8,128]{1,0:T(8,128)S(1)} %get-tuple-element.57.kept, f32[8,128]{1,0:T(8,128)S(1)} %collective-permute-done.10.got, f32[8,128]{1,0:T(8,128)S(1)} %bitcast.40), custom_call_target="tpu_custom_call" | custom-call | flops 100000000 | tf_op jit(solution)/shard_map/pallas_call | solution.py:423
  (2 shorter events, 0.1 us)
Async XLA Ops:
  3.4 21.8 %collective-permute-start = (f32[10,3,32,128]{3,2,1,0:T(8,128)S(1)}, f32[10,3,32,128]{3,2,1,0:T(8,128)S(1)}, u32[]{:S(2)}, u32[]{:S(2)}) collective-permute-start(f32[10,3,32,128]{3,2,1,0:T(8,128)S(1)} %get-tuple-element.33), channel_id=1, source_target_pairs={{0,24},{8,0},{16,8},{24,16},{1,25},{9,1},{17,9},{25,17},{2,26},{10... | collective-permute-start | bytes 1474568 | tf_op jit(solution)/shard_map/ppermute | solution.py:469
  4.1 11.4 %collective-permute-start.4 = (f32[40,8,128]{2,1,0:T(8,128)S(1)}, f32[40,8,128]{2,1,0:T(8,128)S(1)}, u32[]{:S(2)}, u32[]{:S(2)}) collective-permute-start(f32[40,8,128]{2,1,0:T(8,128)S(1)} %get-tuple-element.42), channel_id=1, source_target_pairs={{0,24},{8,0},{16,8},{24,16},{1,25},{9,1},{17,9},{25,17},{2,26},{10... | collective-permute-start | bytes 491528 | tf_op jit(solution)/shard_map/ppermute | solution.py:468
  5.0 11.5 %collective-permute-start.1 = (f32[10,32,128]{2,1,0:T(8,128)S(1)}, f32[10,32,128]{2,1,0:T(8,128)S(1)}, u32[]{:S(2)}, u32[]{:S(2)}) collective-permute-start(f32[10,32,128]{2,1,0:T(8,128)S(1)} %get-tuple-element.34), channel_id=1, source_target_pairs={{0,8},{8,16},{16,24},{24,0},{1,9},{9,17},{17,25},{25,1},{2,10},{10... | collective-permute-start | bytes 491528 | tf_op jit(solution)/shard_map/ppermute | solution.py:472
  5.8 22.9 %collective-permute-start.2 = (f32[60,8,128]{2,1,0:T(8,128)S(1)}, f32[60,8,128]{2,1,0:T(8,128)S(1)}, u32[]{:S(2)}, u32[]{:S(2)}) collective-permute-start(f32[60,8,128]{2,1,0:T(8,128)S(1)} %get-tuple-element.40), channel_id=1, source_target_pairs={{0,1},{1,0},{2,3},{3,2},{4,5},{5,4},{6,7},{7,6},{8,9},{9,8},{10,11... | collective-permute-start | bytes 737288 | tf_op jit(solution)/shard_map/ppermute | solution.py:470
  7.1 21.7 %collective-permute-start.3 = (f32[60,8,128]{2,1,0:T(8,128)S(1)}, f32[60,8,128]{2,1,0:T(8,128)S(1)}, u32[]{:S(2)}, u32[]{:S(2)}) collective-permute-start(f32[60,8,128]{2,1,0:T(8,128)S(1)} %get-tuple-element.41), channel_id=1, source_target_pairs={{1,2},{2,1},{3,4},{4,3},{5,6},{6,5},{0,8},{7,15},{9,10},{10,9},{11... | collective-permute-start | bytes 737288 | tf_op jit(solution)/shard_map/ppermute | solution.py:471
  15.6 3.6 %collective-permute-start.5 = (f32[4,8,128]{2,1,0:T(8,128)S(1)}, f32[4,8,128]{2,1,0:T(8,128)S(1)}, u32[]{:S(2)}, u32[]{:S(2)}) collective-permute-start(f32[4,8,128]{2,1,0:T(8,128)S(1)} %get-tuple-element.45), channel_id=1, source_target_pairs={{0,1},{1,0},{2,3},{3,2},{4,5},{5,4},{6,7},{7,6},{8,9},{9,8},{10,11... | collective-permute-start | bytes 49160 | tf_op jit(solution)/shard_map/ppermute | solution.py:484
  16.6 18.4 %collective-permute-start.7 = (f32[56,8,128]{2,1,0:T(8,128)S(1)}, f32[56,8,128]{2,1,0:T(8,128)S(1)}, u32[]{:S(2)}, u32[]{:S(2)}) collective-permute-start(f32[56,8,128]{2,1,0:T(8,128)S(1)} %get-tuple-element.49), channel_id=1, source_target_pairs={{0,1},{1,0},{2,3},{3,2},{4,5},{5,4},{6,7},{7,6},{8,9},{9,8},{10,11... | collective-permute-start | bytes 688136 | tf_op jit(solution)/shard_map/ppermute | solution.py:486
  19.1 15.9 %collective-permute-start.8 = (f32[56,8,128]{2,1,0:T(8,128)S(1)}, f32[56,8,128]{2,1,0:T(8,128)S(1)}, u32[]{:S(2)}, u32[]{:S(2)}) collective-permute-start(f32[56,8,128]{2,1,0:T(8,128)S(1)} %get-tuple-element.50), channel_id=1, source_target_pairs={{1,2},{2,1},{3,4},{4,3},{5,6},{6,5},{0,8},{7,15},{9,10},{10,9},{11... | collective-permute-start | bytes 688136 | tf_op jit(solution)/shard_map/ppermute | solution.py:487
  25.1 3.7 %collective-permute-start.6 = (f32[4,8,128]{2,1,0:T(8,128)S(1)}, f32[4,8,128]{2,1,0:T(8,128)S(1)}, u32[]{:S(2)}, u32[]{:S(2)}) collective-permute-start(f32[4,8,128]{2,1,0:T(8,128)S(1)} %get-tuple-element.46), channel_id=1, source_target_pairs={{1,2},{2,1},{3,4},{4,3},{5,6},{6,5},{0,8},{7,15},{9,10},{10,9},{11... | collective-permute-start | bytes 49160 | tf_op jit(solution)/shard_map/ppermute | solution.py:485
  28.9 2.8 %collective-permute-start.9 = (f32[16,128]{1,0:T(8,128)S(1)}, f32[16,128]{1,0:T(8,128)S(1)}, u32[]{:S(2)}, u32[]{:S(2)}) collective-permute-start(f32[16,128]{1,0:T(8,128)S(1)} %get-tuple-element.56), channel_id=1, source_target_pairs={{0,16},{8,24},{16,0},{24,8},{1,17},{9,25},{17,1},{25,9},{2,18},{10... | collective-permute-start | bytes 24584 | tf_op jit(solution)/shard_map/ppermute | solution.py:525
  31.7 4.4 %collective-permute-start.10 = (f32[8,128]{1,0:T(8,128)S(1)}, f32[8,128]{1,0:T(8,128)S(1)}, u32[]{:S(2)}, u32[]{:S(2)}) collective-permute-start(f32[8,128]{1,0:T(8,128)S(1)} %get-tuple-element.58), channel_id=1, source_target_pairs={{0,8},{8,0},{16,24},{24,16},{1,9},{9,1},{17,25},{25,17},{2,10},{10... | collective-permute-start | bytes 12296 | tf_op jit(solution)/shard_map/ppermute | solution.py:525
  35.0 1.1 %copy-start = (f32[4,256]{1,0:T(4,128)S(1)}, f32[4,256]{1,0:T(4,128)}, u32[]{:S(2)}) copy-start(f32[4,256]{1,0:T(4,128)} %param.19) | copy-start | bytes 12292
